TPU v7x, 32 devices: a whole 2x2x4 slice. The times are simulated.
32 devices in a mesh: dp: 8 (over y, x, core), grp: 4 (over z).
Axes of the slice: x: 2, y: 2, z: 4, core: 2. Of those that a mesh axis runs over, the one named last changes fastest.
Arguments:
- acts: bfloat16 [192, 32, 2048], P(('dp', 'grp')), may hold values from -6 to 6
- cotan: bfloat16 [192, 32, 1024], P(('dp', 'grp')), may hold values from -0.029907227 to 0.029907227
- lengths: int32 [192], P(('dp', 'grp')), may hold values from 0 to 32, as said below
- offsets: int32 [192], P(('dp', 'grp')), may hold values from 0 to 31, as said below
- kernel: float32 [32, 1024], replicated, may hold values from -1 to 1
- gamma: float32 [1024], replicated, may hold values from 0.1 to 1.9
- beta: float32 [1024], replicated, may hold values from -3 to 3
- w_out: bfloat16 [1024, 1024], replicated, may hold values from -0.1875 to 0.1875
Outputs:
- module_out: bfloat16 [192, 32, 1024], P(('dp', 'grp'))
- grad_w_out: float32 [1024, 1024], P('dp')
- grad_kernel: float32 [32, 1024], P(None, 'dp')
- grad_gamma: float32 [1024], replicated
- grad_beta: float32 [1024], replicated
Inputs may be any that keep to these rules, and one draw needn't show every extreme that they name: `lengths`: each device holds 6 slots; its used slots come first and the others have length 0. A device holds 2 to 6 utterances; the devices with dp indices i and i + 8/2 and the same grp index hold 8 together, and in every draw some such pair holds 6 and 2. Some slot has 32 frames. The utterance of a slot fills frames offsets to offsets + lengths - 1 of that slot.
All inputs are finite; a program needn't handle non-finite values.
Results may differ from a plain program's by a relative error of at most 0.005.
Values may be sent and summed in bfloat16 or wider, within the bound.
No kernel may reach another device: no remote copies, remote signals or barrier semaphores. Data moves between devices by JAX's collectives and lax.ppermute only.
A program may use at most 64 MiB of HBM per device.

v0:
```python
import jax
import jax.numpy as jnp
from jax import lax
from jax.sharding import PartitionSpec as P


def convolve(block_acts, block_len, block_off, kernel):
    taps = kernel.shape[0]
    model_width = kernel.shape[1]
    frame_count = block_acts.shape[1]
    position = jnp.arange(frame_count, dtype=jnp.int32)
    valid = (
        (position[None, :] >= block_off[:, None])
        & (position[None, :] < (block_off + block_len)[:, None])
    ).astype(jnp.float32)
    wide_acts = block_acts.astype(jnp.float32)
    gated = (
        wide_acts[..., :model_width]
        * jax.nn.sigmoid(wide_acts[..., model_width:])
        * valid[..., None]
    )
    padded = jnp.pad(gated, ((0, 0), (taps // 2 - 1, taps // 2), (0, 0)))
    conv_out = padded[:, 0:frame_count] * kernel[0]
    for tap in range(1, taps):
        conv_out = conv_out + padded[:, tap : tap + frame_count] * kernel[tap]
    return (valid, padded, conv_out)


def local(acts, cotan, lengths, offsets, kernel, gamma, beta, w_out):
    model_width = w_out.shape[0]
    taps = kernel.shape[0]
    work_acts, work_cotan, work_len, work_off = (acts, cotan, lengths, offsets)
    valid, padded, conv_out = convolve(work_acts, work_len, work_off, kernel)
    masked = conv_out * valid[..., None]
    sum_first, sum_second, frame_total = lax.psum(
        (
            jnp.sum(masked, axis=(0, 1)),
            jnp.sum(masked * conv_out, axis=(0, 1)),
            jnp.sum(work_len).astype(jnp.float32),
        ),
        ("dp", "grp"),
    )
    mean_value = sum_first / frame_total
    inv_std = lax.rsqrt(sum_second / frame_total - mean_value * mean_value + 1e-05)
    normed = (conv_out - mean_value) * inv_std
    shifted = gamma * normed + beta
    sig_value = jax.nn.sigmoid(shifted)
    hidden = (shifted * sig_value * valid[..., None]).astype(jnp.bfloat16)
    flat_hidden = hidden.reshape(-1, model_width)
    flat_cotan = work_cotan.reshape(-1, model_width)
    outputs = (
        jnp.dot(flat_hidden, w_out, preferred_element_type=jnp.float32)
        .astype(jnp.bfloat16)
        .reshape(work_cotan.shape)
    )
    weight_rows = lax.psum_scatter(
        lax.dot_general(
            flat_hidden, flat_cotan, (((0,), (0,)), ((), ())), preferred_element_type=jnp.float32
        ),
        "dp",
        scatter_dimension=0,
        tiled=True,
    )
    back_hidden = lax.dot_general(
        flat_cotan, w_out, (((1,), (1,)), ((), ())), preferred_element_type=jnp.float32
    ).reshape(conv_out.shape)
    slope = back_hidden * sig_value * (1.0 + shifted * (1.0 - sig_value)) * valid[..., None]
    beta_sum, gamma_sum = lax.psum(
        (jnp.sum(slope, axis=(0, 1)), jnp.sum(slope * normed, axis=(0, 1))), ("dp", "grp")
    )
    conv_grad = (
        gamma
        * inv_std
        * (slope - beta_sum / frame_total - normed * gamma_sum / frame_total)
        * valid[..., None]
    )
    frame_count = conv_out.shape[1]
    kernel_term = jnp.stack(
        [
            jnp.sum(conv_grad * padded[:, tap : tap + frame_count], axis=(0, 1))
            for tap in range(taps)
        ],
        axis=0,
    )
    kernel_cols = kernel_term.T
    kernel_rows = lax.psum_scatter(kernel_cols, "dp", scatter_dimension=0, tiled=True)
    weight_rows, kernel_rows = lax.psum((weight_rows, kernel_rows), "grp")
    return (outputs, weight_rows, kernel_rows.T, gamma_sum, beta_sum)


def solution(mesh):
    placed = (
        P(("dp", "grp"), None, None),
        P(("dp", "grp"), None, None),
        P(("dp", "grp")),
        P(("dp", "grp")),
        P(),
        P(),
        P(),
        P(),
    )
    return jax.shard_map(
        local,
        mesh=mesh,
        in_specs=placed,
        out_specs=(P(("dp", "grp"), None, None), P("dp", None), P(None, "dp"), P(), P()),
        check_vma=False,
    )
```

profile of v0, /device:TPU:0, one launch (start us, length us, event | category | flops | bytes accessed | tf_op | source)
XLA Modules:
  0.0 205.4 jit_solution(17725864448815396489)
XLA Ops:
  7.2 0.0 copy-start
  7.2 0.0 reduce-scatter.3.cloned.1.call-start
  7.2 1.1 fusion.22
  8.4 1.2 fusion.21
  9.6 1.3 fusion.23
  11.6 0.7 fusion.19
  12.3 1.3 convert_element_type.21
  13.6 0.0 copy-start.3
  13.6 0.0 copy-start.5
  13.6 0.2 fusion.16
  13.9 3.9 %fusion.11 = (f32[1024]{0:T(1024)S(1)}, f32[1024]{0:T(1024)S(1)}, f32[6,32,1024]{2,1,0:T(8,128)}) fusion(f32[6,32]{1,0:T(8,128)S(1)} %fusion.19, f32[1024]{0:T(1024)S(1)} %bitcast.151, f32[1024]{0:T(1024)S(1)} %bitcast.152, f32[1024]{0:T(1024)S(1)} %bitcast.122, f32[1024]{0:T(1024)S(1)} %bitcast.123, f32[1024]{0:T(1024)S(1)} %bitcast.124, ...), kind=kLoop, calls=%fused_computation.40 | loop fusion | flops 13170688 | bytes 1712896 | tf_op jit(solution)/shard_map/reduce_sum | solution.py:38
  17.7 42.1 %all-reduce.2 = (f32[1024]{0:T(1024)S(1)}, f32[]{:T(128)}, f32[1024]{0:T(1024)S(1)}) all-reduce(f32[1024]{0:T(1024)S(1)} %get-tuple-element.38, f32[]{:T(128)S(6)} %convert_element_type.23, f32[1024]{0:T(1024)S(1)} %get-tuple-element.37), channel_id=1, replica_groups=mesh['dp'=8,'grp'=4] {'dp','grp'}, use_global_device_ids=true, to_apply=%region_1.2 | all-reduce | flops 2049 | bytes 16392 | tf_op jit(solution)/shard_map/psum | solution.py:35
  59.8 0.0 copy-done.3
  59.8 0.7 fusion.17
  60.5 0.7 add_rsqrt_fusion
  61.1 0.0 copy-done
  61.2 0.0 copy-done.5
  61.2 0.0 copy-start.4
  61.2 3.4 %fusion.20 = (f32[1024]{0:T(1024)S(1)}, f32[1024]{0:T(1024)S(1)}, bf16[6,32,1024]{2,1,0:T(8,128)(2,1)S(1)}, f32[6,32,1024]{2,1,0:T(8,128)}) fusion(f32[1024]{0:T(1024)S(1)} %add_rsqrt_fusion, f32[6,32,1024]{2,1,0:T(8,128)} %get-tuple-element.49, f32[1024]{0:T(1024)S(1)} %get-tuple-element.48, f32[6,32]{1,0:T(8,128)S(1)} %fusion.19, f32[1024]{0:T(1024)S(1)} %copy-done.5, ...), kind=kOutput, calls=%fused_computation.95 | convolution fusion | flops 406386688 | bytes 4481792 | tf_op jit(solution)/shard_map/dot_general | solution.py:64
  64.5 0.0 copy-done.4
  64.5 2.7 %convolution_bitcast_fusion = f32[1024,1024]{1,0:T(8,128)} fusion(bf16[6,32,1024]{2,1,0:T(8,128)(2,1)S(1)} %get-tuple-element.50, bf16[6,32,1024]{2,1,0:T(8,128)(2,1)S(1)} %copy-done.4), kind=kOutput, calls=%fused_computation.31 | convolution fusion | flops 402653184 | bytes 4980736 | tf_op jit(solution)/shard_map/dot_general | solution.py:57
  67.2 0.0 reduce-scatter.3.cloned.1.call-update
  67.3 0.0 reduce-scatter.5.cloned.1.call-start
  67.3 40.7 %all-reduce.1 = (f32[1024]{0:T(1024)S(1)}, f32[1024]{0:T(1024)S(1)}) all-reduce(f32[1024]{0:T(1024)S(1)} %get-tuple-element.40, f32[1024]{0:T(1024)S(1)} %get-tuple-element.39), channel_id=1, replica_groups=mesh['dp'=8,'grp'=4] {'dp','grp'}, use_global_device_ids=true, to_apply=%region_11.12 | all-reduce | flops 2048 | bytes 16384 | tf_op jit(solution)/shard_map/psum | solution.py:68
  108.0 0.0 copy-start.1
  108.0 0.0 copy-start.2
  108.0 0.7 broadcast_divide_fusion
  108.7 4.0 %multiply_reduce_fusion.1 = (f32[1024]{0:T(1024)S(1)}, f32[1024]{0:T(1024)S(1)}, f32[1024]{0:T(1024)S(1)}, f32[1024]{0:T(1024)S(1)}, f32[1024]{0:T(1024)S(1)}, /...) fusion(f32[6,32,1024]{2,1,0:T(8,128)S(1)} %fusion.16, ...), kind=kLoop, calls=%fused_computation.47 | loop fusion | flops 8632320 | bytes 3240708 | tf_op jit(solution)/shard_map/reduce_sum | solution.py:80
  112.7 0.0 copy-done.1
  112.7 0.0 copy-done.2
  112.7 1.4 multiply_reduce_fusion.19
  114.1 2.7 %stack.131 = f32[32,1024]{1,0:T(8,128)} concatenate(f32[1,1024]{1,0:T(1,128)S(1)} %bitcast.120, f32[1,1024]{1,0:T(1,128)S(1)} %bitcast.119, f32[1,1024]{1,0:T(1,128)S(1)} %bitcast.118, f32[1,1024]{1,0:T(1,128)S(1)} %bitcast.117, f32[1,1024]{1,0:T(1,128)S(1)} %bitcast.116, f32[1,1024]{1,0:T(1,128)S(1)} %bitcast.115, f32[1,1024]{1,0:T(1,128)S(1)} %bitcast.114, ...), dimensions={0} | concatenate | bytes 262144 | tf_op jit(solution)/shard_map/stack | solution.py:78
  116.8 0.0 reduce-scatter.5.cloned.1.call-update
  116.8 0.0 all-reduce.5.cloned.1.call-start
  116.9 1.9 reduce-scatter.3.cloned.1.call-done
  118.8 0.0 all-reduce.5.cloned.1.call-update
  118.8 1.3 convolution_convert_fusion
  120.1 35.8 %reduce-scatter.5.cloned.1.call-done = f32[128,32]{0,1:T(8,128)} async-done(((f32[1024,32]{0,1:T(8,128)}), f32[128,32]{0,1:T(8,128)}) %reduce-scatter.5.cloned.1.call-update) | async-done | bytes 16400 | tf_op jit(solution)/shard_map/reduce_scatter | solution.py:86
  156.0 20.0 %psum.55 = f32[32,128]{1,0:T(8,128)} all-reduce(f32[32,128]{1,0:T(8,128)} %bitcast.153), channel_id=1, replica_groups=mesh['dp'=8,'grp'=4] {'grp'}, use_global_device_ids=true, to_apply=%region_45.46 | all-reduce | flops 4096 | bytes 32768 | tf_op jit(solution)/shard_map/psum | solution.py:87
  176.0 21.0 %all-reduce.5.cloned.1.call-done = f32[128,1024]{1,0:T(8,128)} async-done(((f32[128,1024]{1,0:T(8,128)}), f32[128,1024]{1,0:T(8,128)}) %all-reduce.5.cloned.1.call-update) | async-done | bytes 524304 | tf_op jit(solution)/shard_map/psum | solution.py:87
  197.0 1.9 copy.14
Async XLA Ops:
  7.2 54.0 %copy-start = (bf16[1024,1024]{1,0:T(8,128)(2,1)S(1)}, bf16[1024,1024]{1,0:T(8,128)(2,1)}, u32[]{:S(2)}) copy-start(bf16[1024,1024]{1,0:T(8,128)(2,1)} %param.15) | copy-start | bytes 6291460
  7.2 111.6 %reduce-scatter.3.cloned.1.call-start = ((), (), s32[]{:S(2)}) async-start(), calls=%async_computation.2 | async-start | bytes 4718592 | tf_op jit(solution)/shard_map/reduce_scatter | solution.py:56
  13.6 46.2 %copy-start.3 = (f32[1024]{0:T(1024)S(1)}, f32[1024]{0:T(1024)}, u32[]{:S(2)}) copy-start(f32[1024]{0:T(1024)} %param.13) | copy-start | bytes 12292
  13.6 47.5 %copy-start.5 = (f32[1024]{0:T(1024)S(1)}, f32[1024]{0:T(1024)}, u32[]{:S(2)}) copy-start(f32[1024]{0:T(1024)} %param.14) | copy-start | bytes 12292
  61.2 3.4 %copy-start.4 = (bf16[6,32,1024]{2,1,0:T(8,128)(2,1)S(1)}, bf16[6,32,1024]{2,1,0:T(8,128)(2,1)}, u32[]{:S(2)}) copy-start(bf16[6,32,1024]{2,1,0:T(8,128)(2,1)} %param.9) | copy-start | bytes 1179652
  67.3 88.7 %reduce-scatter.5.cloned.1.call-start = ((), (), s32[]{:S(2)}) async-start(), calls=%async_computation.4 | async-start | bytes 147456 | tf_op jit(solution)/shard_map/reduce_scatter | solution.py:86
  108.0 4.7 %copy-start.1 = (f32[1024]{0:T(1024)}, f32[1024]{0:T(1024)S(1)}, u32[]{:S(2)}) copy-start(f32[1024]{0:T(1024)S(1)} %get-tuple-element.89) | copy-start | bytes 12292
  108.0 4.7 %copy-start.2 = (f32[1024]{0:T(1024)}, f32[1024]{0:T(1024)S(1)}, u32[]{:S(2)}) copy-start(f32[1024]{0:T(1024)S(1)} %get-tuple-element.90) | copy-start | bytes 12292
  116.8 80.1 %all-reduce.5.cloned.1.call-start = ((), (), s32[]{:S(2)}) async-start(), calls=%async_computation.3 | async-start | bytes 1048576 | tf_op jit(solution)/shard_map/psum | solution.py:87
Sparse Core Ops, SparseCore 0:
  67.4 51.3 reduce-scatter.2
  122.3 33.5 reduce-scatter.4
  158.3 38.6 all-reduce.4
where the time goes:
time: 206 us; the launch traced here: 205 us
  blocking collectives  103 us (50%)
  waiting for transfers between devices  58.8 us (29%)
  other arithmetic  14.8 us (7%)
  between operations  14.5 us (7%)
  matrix products  7.38 us (4%)
  local copies, waits for them, and re-layouts  6.96 us (3%)
    psum x1, blocking collectives, local(): lax.psum((jnp.sum(masked, axis=(0, 1)), jnp.sum(masked * conv_out, axis=(...  42.1 us
    psum x1, blocking collectives, local(): lax.psum((jnp.sum(slope, axis=(0, 1)), jnp.sum(slope * normed, axis=(0, 1...  40.7 us
    reduce_scatter x1, waiting for transfers between devices, local(): lax.psum_scatter(kernel_cols, 'dp', scatter_dimension=0, tiled=True)  35.8 us
    psum x1, waiting for transfers between devices, local(): weight_rows, kernel_rows = lax.psum((weight_rows, kernel_rows), 'grp')  21 us
    psum x1, blocking collectives, local(): weight_rows, kernel_rows = lax.psum((weight_rows, kernel_rows), 'grp')  20 us
    reduce_sum x2, other arithmetic, local(): jnp.sum(conv_grad * padded[:, tap:tap + frame_count], axis=(0, 1))  5.41 us
  transfers between devices with their start and end apart: 3, of which 3 were waited for; matrix products, arithmetic and copies ran while one was open for 5% of the time, Pallas kernels for 0%

commit v1 on v0

--- a/solution.py
+++ b/solution.py
@@ -1,7 +1,16 @@
+import functools
+
 import jax
 import jax.numpy as jnp
 from jax import lax
+from jax.experimental import pallas as pl
+from jax.experimental.pallas import tpu as pltpu
 from jax.sharding import PartitionSpec as P
+
+
+LANES = 128
+F32 = jnp.float32
+BF16 = jnp.bfloat16
 
 
 def convolve(block_acts, block_len, block_off, kernel):
@@ -26,17 +35,16 @@
     return (valid, padded, conv_out)
 
 
-def local(acts, cotan, lengths, offsets, kernel, gamma, beta, w_out):
+def local_general(acts, cotan, lengths, offsets, kernel, gamma, beta, w_out):
     model_width = w_out.shape[0]
     taps = kernel.shape[0]
-    work_acts, work_cotan, work_len, work_off = (acts, cotan, lengths, offsets)
-    valid, padded, conv_out = convolve(work_acts, work_len, work_off, kernel)
+    valid, padded, conv_out = convolve(acts, lengths, offsets, kernel)
     masked = conv_out * valid[..., None]
     sum_first, sum_second, frame_total = lax.psum(
         (
             jnp.sum(masked, axis=(0, 1)),
             jnp.sum(masked * conv_out, axis=(0, 1)),
-            jnp.sum(work_len).astype(jnp.float32),
+            jnp.sum(lengths).astype(jnp.float32),
         ),
         ("dp", "grp"),
     )
@@ -47,11 +55,11 @@
     sig_value = jax.nn.sigmoid(shifted)
     hidden = (shifted * sig_value * valid[..., None]).astype(jnp.bfloat16)
     flat_hidden = hidden.reshape(-1, model_width)
-    flat_cotan = work_cotan.reshape(-1, model_width)
+    flat_cotan = cotan.reshape(-1, model_width)
     outputs = (
         jnp.dot(flat_hidden, w_out, preferred_element_type=jnp.float32)
         .astype(jnp.bfloat16)
-        .reshape(work_cotan.shape)
+        .reshape(cotan.shape)
     )
     weight_rows = lax.psum_scatter(
         lax.dot_general(
@@ -82,13 +90,420 @@
         ],
         axis=0,
     )
-    kernel_cols = kernel_term.T
-    kernel_rows = lax.psum_scatter(kernel_cols, "dp", scatter_dimension=0, tiled=True)
+    kernel_rows = lax.psum_scatter(kernel_term.T, "dp", scatter_dimension=0, tiled=True)
     weight_rows, kernel_rows = lax.psum((weight_rows, kernel_rows), "grp")
     return (outputs, weight_rows, kernel_rows.T, gamma_sum, beta_sum)
 
 
+def mask_of(len_ref, off_ref, slot, frames):
+    length, offset = len_ref[slot], off_ref[slot]
+    position = lax.broadcasted_iota(jnp.int32, (frames, LANES), 0)
+    return ((position >= offset) & (position < offset + length)).astype(F32)
+
+
+def fold(value):
+    total = value[0:8]
+    for at in range(8, value.shape[0], 8):
+        total = total + value[at : at + 8]
+    return total
+
+
+def row_sum(value):
+    return jnp.sum(value, axis=0, keepdims=True)
+
+
+def conv_body(len_ref, off_ref, acts_ref, k_ref, gp_ref, cv_ref, st_ref, acc_ref):
+    _, frames, wide = acts_ref.shape
+    blocks, slots, rows, _ = gp_ref.shape
+    taps = k_ref.shape[0]
+    lead = taps // 2
+    slot = pl.program_id(0)
+
+    @pl.when(slot == 0)
+    def _():
+        acc_ref[...] = jnp.zeros_like(acc_ref)
+
+    valid = mask_of(len_ref, off_ref, slot, frames)
+    for block in range(blocks):
+        cols = slice(block * LANES, (block + 1) * LANES)
+        gate = slice(wide // 2 + block * LANES, wide // 2 + (block + 1) * LANES)
+        left, right = acts_ref[0, :, cols].astype(F32), acts_ref[0, :, gate].astype(F32)
+        gp_ref[block, slot, 0:lead, :] = jnp.zeros((lead, LANES), F32)
+        gp_ref[block, slot, lead : lead + frames, :] = left * jax.nn.sigmoid(right) * valid
+        gp_ref[block, slot, lead + frames : rows, :] = jnp.zeros((rows - lead - frames, LANES), F32)
+    for block in range(blocks):
+        cols = slice(block * LANES, (block + 1) * LANES)
+        total = gp_ref[block, slot, 1 : 1 + frames, :] * k_ref[0:1, cols]
+        for tap in range(1, taps):
+            total = total + gp_ref[block, slot, 1 + tap : 1 + tap + frames, :] * k_ref[tap : tap + 1, cols]
+        cv_ref[block, slot] = total
+        masked = total * valid
+        acc_ref[0, block] += fold(masked)
+        acc_ref[1, block] += fold(masked * total)
+
+    @pl.when(slot == slots - 1)
+    def _():
+        for block in range(blocks):
+            cols = slice(block * LANES, (block + 1) * LANES)
+            st_ref[0:1, cols] = row_sum(acc_ref[0, block])
+            st_ref[1:2, cols] = row_sum(acc_ref[1, block])
+        count = len_ref[0]
+        for other in range(1, slots):
+            count = count + len_ref[other]
+        st_ref[:, blocks * LANES :] = jnp.full((2, LANES), count.astype(F32), F32)
+
+
+def lag_sums(gp_ref, block, weights, taps, group, put):
+    frames = weights(0).shape[0]
+    slots = gp_ref.shape[1]
+    for low in range(0, taps, group):
+        sums = [None] * group
+        for slot in range(slots):
+            weight = weights(slot)
+            for j in range(group):
+                at = 1 + low + j
+                term = fold(weight * gp_ref[block, slot, at : at + frames, :])
+                sums[j] = term if sums[j] is None else sums[j] + term
+        for j in range(group):
+            put(low + j, row_sum(sums[j]))
+
+
+def aux_body(start, len_ref, off_ref, gp_ref, cv_ref, out_ref, wt_ref):
+    _, slots, frames, _ = cv_ref.shape
+    many, _, taps, _ = out_ref.shape
+    lead = taps // 2
+    lag = lax.broadcasted_iota(jnp.int32, (taps, frames), 0)
+    at = lax.broadcasted_iota(jnp.int32, (taps, frames), 1) - lag + (lead - 1)
+
+    def one(i, carry):
+        block = start + i
+        for slot in range(slots):
+            wt_ref[slot] = cv_ref[block, slot] * mask_of(len_ref, off_ref, slot, frames)
+
+        def put(k, row):
+            out_ref[i, 0, k : k + 1, :] = row
+
+        lag_sums(gp_ref, block, lambda slot: wt_ref[slot], taps, 16, put)
+        total = jnp.zeros((taps, LANES), F32)
+        for slot in range(slots):
+            inside = (
+                (at >= off_ref[slot])
+                & (at < off_ref[slot] + len_ref[slot])
+                & (at >= 0)
+                & (at < frames)
+            ).astype(BF16)
+            rest = gp_ref[block, slot, lead : lead + frames, :]
+            for _ in range(3):
+                part = rest.astype(BF16)
+                rest = rest - part.astype(F32)
+                total = total + jnp.dot(inside, part, preferred_element_type=F32)
+        out_ref[i, 1] = total
+        return carry
+
+    lax.fori_loop(0, many, one, 0)
+
+
+def back_body(cotan_ref, w_ref, out_ref):
+    for block in range(out_ref.shape[0]):
+        rows = w_ref[block * LANES : (block + 1) * LANES, :]
+        out_ref[block] = lax.dot_general(
+            cotan_ref[...], rows, (((1,), (1,)), ((), ())), preferred_element_type=F32
+        )
+
+
+def scale_of(st_ref, block):
+    width = st_ref.shape[1] - LANES
+    cols = pl.ds(pl.multiple_of(block * LANES, LANES), LANES)
+    count = st_ref[0:1, width:]
+    mean = st_ref[0:1, cols] / count
+    inv = lax.rsqrt(st_ref[1:2, cols] / count - mean * mean + 1e-05)
+    return count, mean, inv
+
+
+def hidden_body(len_ref, off_ref, st_ref, g_ref, b_ref, cv_ref, hid_ref):
+    blocks, slots, frames, _ = cv_ref.shape
+
+    def one(block, carry):
+        _, mean, inv = scale_of(st_ref, block)
+        gain, shift = g_ref[pl.ds(block, 1), :], b_ref[pl.ds(block, 1), :]
+        for slot in range(slots):
+            valid = mask_of(len_ref, off_ref, slot, frames)
+            shifted = gain * ((cv_ref[block, slot] - mean) * inv) + shift
+            hidden = shifted * jax.nn.sigmoid(shifted) * valid
+            hid_ref[block, slot * frames : (slot + 1) * frames, :] = hidden.astype(BF16)
+        return carry
+
+    lax.fori_loop(0, blocks, one, 0)
+
+
+def slope_body(len_ref, off_ref, st_ref, g_ref, b_ref, gp_ref, cv_ref, bk_ref, *refs):
+    aux_refs, q_ref, sl_ref = refs[:-2], refs[-2], refs[-1]
+    _, slots, frames, _ = cv_ref.shape
+    taps = aux_refs[0].shape[2]
+    each = aux_refs[0].shape[0]
+
+    def one(block, aux_ref, i):
+        _, mean, inv = scale_of(st_ref, block)
+        gain, shift = g_ref[pl.ds(block, 1), :], b_ref[pl.ds(block, 1), :]
+        first = second = jnp.zeros((8, LANES), F32)
+        for slot in range(slots):
+            valid = mask_of(len_ref, off_ref, slot, frames)
+            normed = (cv_ref[block, slot] - mean) * inv
+            shifted = gain * normed + shift
+            sig = jax.nn.sigmoid(shifted)
+            back = bk_ref[block, slot * frames : (slot + 1) * frames, :]
+            slope = back * sig * (1.0 + shifted * (1.0 - sig)) * valid
+            sl_ref[slot] = slope
+            first, second = first + fold(slope), second + fold(slope * normed)
+
+        def put(k, row):
+            q_ref[block, k : k + 1, :] = row
+
+        lag_sums(gp_ref, block, lambda slot: sl_ref[slot], taps, 16, put)
+        q_ref[block, taps : 2 * taps, :] = aux_ref[i, 1]
+        q_ref[block, 2 * taps : 3 * taps, :] = inv * (aux_ref[i, 0] - mean * aux_ref[i, 1])
+        q_ref[block, 3 * taps : 3 * taps + 1, :] = row_sum(first)
+        q_ref[block, 3 * taps + 1 : 3 * taps + 2, :] = row_sum(second)
+        left = q_ref.shape[1] - 3 * taps - 2
+        q_ref[block, 3 * taps + 2 :, :] = jnp.zeros((left, LANES), F32)
+
+    for part, aux_ref in enumerate(aux_refs):
+
+        def step(i, carry, part=part, aux_ref=aux_ref):
+            one(part * each + i, aux_ref, i)
+            return carry
+
+        lax.fori_loop(0, each, step, 0)
+
+
+def out_body(hid_ref, w_ref, out_ref):
+    blocks = hid_ref.shape[0]
+    slots, frames, _ = out_ref.shape
+    total = None
+    for block in range(blocks):
+        term = jnp.dot(
+            hid_ref[block],
+            w_ref[block * LANES : (block + 1) * LANES, :],
+            preferred_element_type=F32,
+        )
+        total = term if total is None else total + term
+    for slot in range(slots):
+        out_ref[slot] = total[slot * frames : (slot + 1) * frames, :].astype(BF16)
+
+
+def rows_body(masks, flip, at_ref, recv_ref, *refs):
+    pieces, out_ref = refs[:-1], refs[-1]
+    me = at_ref[0]
+    half = 1 - at_ref[1] if flip else at_ref[1]
+    width = pieces[0].shape[1] // 2
+    cols = pl.ds(pl.multiple_of(half * width, width), width)
+    total = None
+    for mask, piece in zip(masks, pieces):
+        left = recv_ref[jnp.bitwise_xor(me, mask)]
+        term = lax.dot_general(
+            left, piece[:, cols], (((0,), (0,)), ((), ())), preferred_element_type=F32
+        )
+        total = term if total is None else total + term
+    for block in range(width // LANES):
+        out_ref[block] = total[:, block * LANES : (block + 1) * LANES].astype(BF16)
+
+
+def add_body(own_ref, recv_ref, out_ref):
+    out_ref[...] = (own_ref[...].astype(F32) + recv_ref[...].astype(F32)).astype(out_ref.dtype)
+
+
+def sum_body(recv_ref, out_ref):
+    total = recv_ref[0]
+    for source in range(1, recv_ref.shape[0]):
+        total = total + recv_ref[source]
+    out_ref[...] = total
+
+
+def last_body(taps, at_ref, own_ref, recv_ref, st_ref, g_ref, gk_ref, gs_ref):
+    me = at_ref[0]
+    value = own_ref[...] + recv_ref[...]
+    count, _, inv = scale_of(st_ref, me)
+    beta_sum = value[3 * taps : 3 * taps + 1]
+    gamma_sum = value[3 * taps + 1 : 3 * taps + 2]
+    gk_ref[...] = (g_ref[pl.ds(me, 1), :] * inv) * (
+        value[0:taps]
+        - (beta_sum / count) * value[taps : 2 * taps]
+        - (gamma_sum / count) * value[2 * taps : 3 * taps]
+    )
+    gs_ref[...] = jnp.zeros_like(gs_ref)
+    cols = pl.ds(pl.multiple_of(me * LANES, LANES), LANES)
+    gs_ref[0:1, cols] = gamma_sum
+    gs_ref[1:2, cols] = beta_sum
+
+
+def spread_body(at_ref, own_ref, recv_ref, out_ref):
+    half = at_ref[1]
+    many = own_ref.shape[0]
+    for which, ref in ((half, own_ref), (1 - half, recv_ref)):
+        for block in range(many):
+            cols = pl.ds(pl.multiple_of((which * many + block) * LANES, LANES), LANES)
+            out_ref[:, cols] = ref[block].astype(F32)
+
+
+SMEM = pl.BlockSpec(memory_space=pltpu.SMEM)
+VMEM = pl.BlockSpec(memory_space=pltpu.VMEM)
+
+
+def call(body, shapes, scalars, args, flops=0, scratch=(), mib=8, **more):
+    many = isinstance(shapes, list)
+    moved = sum(a.size * a.dtype.itemsize for a in args)
+    return pl.pallas_call(
+        body,
+        in_specs=more.pop("in_specs", None) or [SMEM] * len(scalars) + [VMEM] * len(args),
+        out_specs=[VMEM] * len(shapes) if many else VMEM,
+        out_shape=shapes,
+        scratch_shapes=scratch,
+        compiler_params=pltpu.CompilerParams(vmem_limit_bytes=mib << 20),
+        cost_estimate=pl.CostEstimate(flops=flops, bytes_accessed=moved, transcendentals=0),
+        **more,
+    )(*scalars, *args)
+
+
+def local_fast(n_dp, n_grp, acts, cotan, lengths, offsets, kernel, gamma, beta, w_out):
+    slots, frames, wide = acts.shape
+    width = wide // 2
+    taps = kernel.shape[0]
+    blocks = width // LANES
+    tokens = slots * frames
+    n_q = 3 * taps + 8
+    padded = 2 * (taps // 2) + frames
+    me_dp, me_grp = lax.axis_index("dp"), lax.axis_index("grp")
+    shape = jax.ShapeDtypeStruct
+
+    def swap(value, dp_mask, grp_mask):
+        pairs = [
+            (d * n_grp + g, (d ^ dp_mask) * n_grp + (g ^ grp_mask))
+            for d in range(n_dp)
+            for g in range(n_grp)
+        ]
+        return lax.ppermute(value, ("dp", "grp"), pairs)
+
+    dp_bits = [1 << i for i in range(n_dp.bit_length() - 1)]
+    grp_bits = [1 << i for i in range(n_grp.bit_length() - 1)]
+    at = jnp.stack([me_dp, me_grp % 2]).astype(jnp.int32)
+    gamma2, beta2 = gamma.reshape(blocks, LANES), beta.reshape(blocks, LANES)
+
+    flat_cotan = cotan.reshape(tokens, width)
+    pieces = [(0, flat_cotan)]
+    for bit in dp_bits[1:] + dp_bits[:1]:
+        pieces += [(m | bit, swap(v, bit, 0)) for m, v in pieces]
+    masks, values = tuple(m for m, _ in pieces), [v for _, v in pieces]
+
+    gated, conv_out, stats = call(
+        conv_body,
+        [
+            shape((blocks, slots, padded, LANES), F32),
+            shape((blocks, slots, frames, LANES), F32),
+            shape((2, width + LANES), F32),
+        ],
+        (lengths, offsets),
+        (acts, kernel),
+        flops=4 * taps * tokens * width,
+        scratch=[pltpu.VMEM((2, blocks, 8, LANES), F32)],
+        grid=(slots,),
+        in_specs=[SMEM, SMEM, pl.BlockSpec((1, frames, wide), lambda s: (s, 0, 0)), VMEM],
+    )
+
+    hops = [(1, m) for m in grp_bits] + [(m | 1, 0) for m in dp_bits[1:]] + [(1, 0)]
+    for dp_mask, grp_mask in hops:
+        stats = stats + swap(stats, dp_mask, grp_mask)
+
+    back = call(
+        back_body,
+        shape((blocks, tokens, LANES), F32),
+        (),
+        (flat_cotan, w_out),
+        flops=2 * tokens * width * width,
+    )
+    parts = 4
+    while blocks % parts:
+        parts //= 2
+    each = blocks // parts
+    aux = [
+        call(
+            functools.partial(aux_body, i * each),
+            shape((each, 2, taps, LANES), F32),
+            (lengths, offsets),
+            (gated, conv_out),
+            flops=4 * taps * tokens * each * LANES,
+            scratch=[pltpu.VMEM((slots, frames, LANES), F32)],
+        )
+        for i in range(parts)
+    ]
+
+    hidden = call(
+        hidden_body,
+        shape((blocks, tokens, LANES), BF16),
+        (lengths, offsets),
+        (stats, gamma2, beta2, conv_out),
+    )
+    received = lax.all_to_all(hidden, "dp", 0, 0, tiled=True)
+    lags = call(
+        slope_body,
+        shape((blocks, n_q, LANES), F32),
+        (lengths, offsets),
+        (stats, gamma2, beta2, gated, conv_out, back, *aux),
+        flops=4 * taps * tokens * width,
+        scratch=[pltpu.VMEM((slots, frames, LANES), F32)],
+    )
+    lags = lax.all_to_all(lags, "dp", 0, 0, tiled=True)
+    outputs = call(out_body, shape(cotan.shape, BF16), (), (hidden, w_out))
+
+    half_shape = shape((blocks // 2, LANES, LANES), BF16)
+    flops = n_dp * tokens * LANES * width
+
+    def rows_of(flip):
+        body = functools.partial(rows_body, masks, flip)
+        return call(body, half_shape, (at,), (received, *values), flops=flops)
+
+    given = rows_of(True)
+    taken = swap(given, 0, 1)
+    kept = rows_of(False)
+    both = call(add_body, half_shape, (), (kept, taken))
+    for mask in grp_bits[1:]:
+        both = call(add_body, half_shape, (), (both, swap(both, 0, mask)))
+    rest = swap(both, 0, 1)
+
+    lags = call(sum_body, shape((n_q, LANES), F32), (), (lags,))
+    for mask in grp_bits[:-1]:
+        lags = lags + swap(lags, 0, mask)
+    grad_kernel, small = call(
+        functools.partial(last_body, taps),
+        [shape((taps, LANES), F32), shape((2, width), F32)],
+        (at,),
+        (lags, swap(lags, 0, grp_bits[-1]), stats, gamma2),
+    )
+    for mask in dp_bits[1:] + [0]:
+        small = small + swap(small, mask | 1, 0)
+    weight_rows = call(spread_body, shape((LANES, width), F32), (at,), (both, rest))
+    return (outputs, weight_rows, grad_kernel, small[0], small[1])
+
+
 def solution(mesh):
+    n_dp, n_grp = mesh.shape["dp"], mesh.shape["grp"]
+
+    def fits(width, taps, frames):
+        return (
+            n_dp & (n_dp - 1) == 0
+            and n_grp & (n_grp - 1) == 0
+            and n_dp >= 4
+            and n_grp >= 4
+            and width == n_dp * LANES
+            and taps % 16 == 0
+            and frames % 16 == 0
+        )
+
+    def local(acts, cotan, lengths, offsets, kernel, gamma, beta, w_out):
+        args = (acts, cotan, lengths, offsets, kernel, gamma, beta, w_out)
+        if not fits(w_out.shape[0], kernel.shape[0], acts.shape[1]):
+            return local_general(*args)
+        return local_fast(n_dp, n_grp, *args)
+
     placed = (
         P(("dp", "grp"), None, None),
         P(("dp", "grp"), None, None),

time: 206 us -> 98.9 us (0.48)
  blocking collectives: 103 us -> 0 us
  starting transfers between devices: 0.12 us -> 29.1 us
  Pallas kernels: 0 us -> 22.7 us
  waiting for transfers between devices: 58.8 us -> 37.4 us
  other arithmetic: 14.8 us -> 0.13 us
  between operations: 14.5 us -> 0.92 us
  matrix products: 7.38 us -> 0 us
    psum x3 -> x0, blocking collectives: 103 us -> none  [the longest x1 42.1 us: local(): lax.psum((jnp.sum(masked, axis=(0, 1)), jnp.sum(masked * conv_out, axis=(...]
    reduce_scatter x2 -> x0, waiting for transfers between devices: 37.7 us -> none  [the longest x1 35.8 us: local(): lax.psum_scatter(kernel_cols, 'dp', scatter_dimension=0, tiled=True)]
    ppermute x0 -> x20, waiting for transfers between devices: none -> 32.6 us  [swap(): return lax.ppermute(value, ('dp', 'grp'), pairs)]
    pallas_call x0 -> x16, Pallas kernels: none -> 22.7 us  [call(): pl.pallas_call(body, in_specs=more.pop('in_specs', None) or [SMEM] * len(...]
    ppermute x0 -> x20, starting transfers between devices: none -> 21.6 us  [swap(): return lax.ppermute(value, ('dp', 'grp'), pairs)]
    psum x1 -> x0, waiting for transfers between devices: 21 us -> none  [local(): weight_rows, kernel_rows = lax.psum((weight_rows, kernel_rows), 'grp')]
    reduce_sum x4 -> x0, other arithmetic: 10.6 us -> none  [the longest x2 5.41 us: local(): jnp.sum(conv_grad * padded[:, tap:tap + frame_count], axis=(0, 1))]
    all_to_all x0 -> x2, starting transfers between devices: none -> 7.51 us  [the longest x1 4.06 us: local_fast(): lags = lax.all_to_all(lags, 'dp', 0, 0, tiled=True)]
  transfers between devices with their start and end apart: 3 -> 22, of which waited for: 3 -> 11; matrix products, arithmetic and copies ran while one was open for 5% -> 1% of each run, Pallas kernels for 0% -> 22%
where the time goes in v1:
time: 98.9 us; the launch traced here: 98.4 us
  waiting for transfers between devices  37.4 us (38%)
  starting transfers between devices  29.1 us (29%)
  Pallas kernels  22.7 us (23%)
  local copies, waits for them, and re-layouts  8.08 us (8%)
    ppermute x20, waiting for transfers between devices, swap(): return lax.ppermute(value, ('dp', 'grp'), pairs)  32.6 us
    pallas_call x16, Pallas kernels, call(): pl.pallas_call(body, in_specs=more.pop('in_specs', None) or [SMEM] * len(...  22.7 us
    ppermute x20, starting transfers between devices, swap(): return lax.ppermute(value, ('dp', 'grp'), pairs)  21.6 us
    unnamed x36, local copies, waits for them, and re-layouts  7.47 us
    all_to_all x1, waiting for transfers between devices, local_fast(): lags = lax.all_to_all(lags, 'dp', 0, 0, tiled=True)  4.82 us
    all_to_all x1, starting transfers between devices, local_fast(): lags = lax.all_to_all(lags, 'dp', 0, 0, tiled=True)  4.06 us
    all_to_all x1, starting transfers between devices, local_fast(): received = lax.all_to_all(hidden, 'dp', 0, 0, tiled=True)  3.45 us
  transfers between devices with their start and end apart: 22, of which 11 were waited for; matrix products, arithmetic and copies ran while one was open for 1% of the time, Pallas kernels for 22%

profile of v1, /device:TPU:0, one launch (start us, length us, event | category | flops | bytes accessed | tf_op | source)
XLA Modules:
  0.0 98.4 jit_solution(11808514128083159142)
XLA Ops:
  0.6 3.0 %collective-permute-start.5 = (bf16[192,1024]{1,0:T(8,128)(2,1)}, bf16[192,1024]{1,0:T(8,128)(2,1)S(1)}, u32[]{:S(2)}, u32[]{:S(2)}) collective-permute-start(bf16[192,1024]{1,0:T(8,128)(2,1)} %bitcast.7), channel_id=1, source_target_pairs={{0,8},{1,9},{2,10},{3,11},{4,12},{5,13},{6,14},{7,15},{8,0},{9,1},... | collective-permute-start | bytes 1179656 | tf_op jit(solution)/shard_map/ppermute | solution.py:384
  3.7 1.5 %collective-permute-start.6 = (bf16[192,1024]{1,0:T(8,128)(2,1)}, bf16[192,1024]{1,0:T(8,128)(2,1)}, u32[]{:S(2)}, u32[]{:S(2)}) collective-permute-start(bf16[192,1024]{1,0:T(8,128)(2,1)} %bitcast.8), channel_id=1, source_target_pairs={{0,16},{1,17},{2,18},{3,19},{4,20},{5,21},{6,22},{7,23},{8,24},{9,... | collective-permute-start | bytes 1179656 | tf_op jit(solution)/shard_map/ppermute | solution.py:384
  5.2 7.8 %collective-permute-done.5.refs_1_ = bf16[192,1024]{1,0:T(8,128)(2,1)S(1)} collective-permute-done((bf16[192,1024]{1,0:T(8,128)(2,1)}, bf16[192,1024]{1,0:T(8,128)(2,1)S(1)}, u32[]{:S(2)}, u32[]{:S(2)}) %collective-permute-start.5) | collective-permute-done | bytes 393248 | tf_op jit(solution)/shard_map/ppermute | solution.py:384
  13.0 1.8 %collective-permute-start.7 = (bf16[192,1024]{1,0:T(8,128)(2,1)S(1)}, bf16[192,1024]{1,0:T(8,128)(2,1)}, u32[]{:S(2)}, u32[]{:S(2)}) collective-permute-start(bf16[192,1024]{1,0:T(8,128)(2,1)S(1)} %collective-permute-done.5.refs_1_), channel_id=1, source_target_pairs={{0,16},{1,17},{2,18},{3,19},{4,20},{5,21},{6,22},{7,23},{8,24},{9,... | collective-permute-start | bytes 1179656 | tf_op jit(solution)/shard_map/ppermute | solution.py:384
  14.8 1.1 %copy-done.4 = bf16[6,32,2048]{2,1,0:T(8,128)(2,1)S(1)} copy-done((bf16[6,32,2048]{2,1,0:T(8,128)(2,1)S(1)}, bf16[6,32,2048]{2,1,0:T(8,128)(2,1)}, u32[]{:S(2)}) %copy-start.4) | copy-done | bytes 786456
  15.9 0.9 copy-done.5
  16.8 0.7 copy-done.8
  17.5 0.7 copy-done.12
  18.1 2.6 %shard_map.119 = (f32[8,6,64,128]{3,2,1,0:T(8,128)S(1)}, f32[8,6,32,128]{3,2,1,0:T(8,128)S(1)}, f32[2,1152]{1,0:T(2,128)S(1)}) custom-call(s32[6]{0:T(128)S(1)} %copy-done.8, s32[6]{0:T(128)S(1)} %copy-done.12, bf16[6,32,2048]{2,1,0:T(8,128)(2,1)S(1)} %copy-done.4, f32[32,1024]{1,0:T(8,128)S(1)} %copy-done.5), custom_call_target="tpu_custom_call" | custom-call | flops 25165824 | bytes 917504 | tf_op jit(solution)/shard_map/pallas_call | solution.py:355
  20.8 3.1 %collective-permute-done = f32[2,1152]{1,0:T(2,128)S(1)} collective-permute-done((f32[2,1152]{1,0:T(2,128)S(1)}, f32[2,1152]{1,0:T(2,128)S(1)}, u32[]{:S(2)}, u32[]{:S(2)}) %collective-permute-start) | collective-permute-done | bytes 9248 | tf_op jit(solution)/shard_map/ppermute | solution.py:384
  23.9 2.3 %collective-permute-start.1 = (f32[2,1152]{1,0:T(2,128)S(1)}, f32[2,1152]{1,0:T(2,128)S(1)}, u32[]{:S(2)}, u32[]{:S(2)}) collective-permute-start(f32[2,1152]{1,0:T(2,128)S(1)} %add.31), channel_id=1, source_target_pairs={{0,6},{1,7},{2,4},{3,5},{4,2},{5,3},{6,0},{7,1},{8,14},{9,15},{10,... | collective-permute-start | bytes 27656 | tf_op jit(solution)/shard_map/ppermute | solution.py:384
  26.2 1.7 %collective-permute-done.1 = f32[2,1152]{1,0:T(2,128)S(1)} collective-permute-done((f32[2,1152]{1,0:T(2,128)S(1)}, f32[2,1152]{1,0:T(2,128)S(1)}, u32[]{:S(2)}, u32[]{:S(2)}) %collective-permute-start.1) | collective-permute-done | bytes 9248 | tf_op jit(solution)/shard_map/ppermute | solution.py:384
  27.9 1.2 %collective-permute-start.2 = (f32[2,1152]{1,0:T(2,128)S(1)}, f32[2,1152]{1,0:T(2,128)S(1)}, u32[]{:S(2)}, u32[]{:S(2)}) collective-permute-start(f32[2,1152]{1,0:T(2,128)S(1)} %add.32), channel_id=1, source_target_pairs={{0,12},{1,13},{2,14},{3,15},{4,8},{5,9},{6,10},{7,11},{8,4},{9,5},... | collective-permute-start | bytes 27656 | tf_op jit(solution)/shard_map/ppermute | solution.py:384
  29.1 1.9 %collective-permute-done.2 = f32[2,1152]{1,0:T(2,128)S(1)} collective-permute-done((f32[2,1152]{1,0:T(2,128)S(1)}, f32[2,1152]{1,0:T(2,128)S(1)}, u32[]{:S(2)}, u32[]{:S(2)}) %collective-permute-start.2) | collective-permute-done | bytes 9248 | tf_op jit(solution)/shard_map/ppermute | solution.py:384
  31.4 2.6 %collective-permute-done.3 = f32[2,1152]{1,0:T(2,128)S(1)} collective-permute-done((f32[2,1152]{1,0:T(2,128)S(1)}, f32[2,1152]{1,0:T(2,128)S(1)}, u32[]{:S(2)}, u32[]{:S(2)}) %collective-permute-start.3) | collective-permute-done | bytes 9248 | tf_op jit(solution)/shard_map/ppermute | solution.py:384
  34.2 1.1 %collective-permute-done.4 = f32[2,1152]{1,0:T(2,128)S(1)} collective-permute-done((f32[2,1152]{1,0:T(2,128)S(1)}, f32[2,1152]{1,0:T(2,128)S(1)}, u32[]{:S(2)}, u32[]{:S(2)}) %collective-permute-start.4) | collective-permute-done | bytes 9248 | tf_op jit(solution)/shard_map/ppermute | solution.py:384
  35.3 0.7 copy-done.6
  35.9 0.7 copy-done.9
  36.6 0.7 copy-done.13
  37.3 0.7 copy-done.16
  37.9 1.7 %shard_map.120.hid_ref = bf16[8,192,128]{2,1,0:T(8,128)(2,1)} custom-call(s32[6]{0:T(128)S(1)} %copy-done.9, s32[6]{0:T(128)S(1)} %copy-done.13, f32[2,1152]{1,0:T(2,128)S(1)} %add.35.st_ref, f32[8,128]{1,0:T(8,128)S(1)} %bitcast.13, f32[8,128]{1,0:T(8,128)S(1)} %bitcast.16, f32[8,6,32,128]{3,2,1,0:T(8,128)S(1)} %get-tuple-element.11.cv_ref), custom_call_target="tpu_custom_call" | custom-call | bytes 803840 | tf_op jit(solution)/shard_map/pallas_call | solution.py:355
  39.7 3.5 %all-to-all-start = ((bf16[8,192,128]{2,1,0:T(8,128)(2,1)}), bf16[8,192,128]{2,1,0:T(8,128)(2,1)S(1)}, u32[]{:S(2)}, u32[]{:S(2)}) async-start(bf16[8,192,128]{2,1,0:T(8,128)(2,1)} %shard_map.120.hid_ref), calls=%async_computation | async-start | bytes 786432 | tf_op jit(solution)/shard_map/all_to_all | solution.py:445
  44.2 0.7 copy-done.14
  44.9 1.2 %shard_map.128.refs_0_ = f32[2,2,32,128]{3,2,1,0:T(8,128)S(1)} custom-call(s32[6]{0:T(128)S(1)} %copy-done.10, s32[6]{0:T(128)S(1)} %copy-done.14, f32[8,6,64,128]{3,2,1,0:T(8,128)S(1)} %get-tuple-element.12.gp_ref, f32[8,6,32,128]{3,2,1,0:T(8,128)S(1)} %get-tuple-element.11.cv_ref), custom_call_target="tpu_custom_call" | custom-call | flops 6291456 | bytes 2359296 | tf_op jit(solution)/shard_map/pallas_call | solution.py:355
  46.1 1.2 %shard_map.129.refs_1_ = f32[2,2,32,128]{3,2,1,0:T(8,128)S(1)} custom-call(s32[6]{0:T(128)S(1)} %copy-done.10, s32[6]{0:T(128)S(1)} %copy-done.14, f32[8,6,64,128]{3,2,1,0:T(8,128)S(1)} %get-tuple-element.12.gp_ref, f32[8,6,32,128]{3,2,1,0:T(8,128)S(1)} %get-tuple-element.11.cv_ref), custom_call_target="tpu_custom_call" | custom-call | flops 6291456 | bytes 2359296 | tf_op jit(solution)/shard_map/pallas_call | solution.py:355
  47.4 1.2 %shard_map.130.refs_2_ = f32[2,2,32,128]{3,2,1,0:T(8,128)S(1)} custom-call(s32[6]{0:T(128)S(1)} %copy-done.10, s32[6]{0:T(128)S(1)} %copy-done.15, f32[8,6,64,128]{3,2,1,0:T(8,128)S(1)} %get-tuple-element.12.gp_ref, f32[8,6,32,128]{3,2,1,0:T(8,128)S(1)} %get-tuple-element.11.cv_ref), custom_call_target="tpu_custom_call" | custom-call | flops 6291456 | bytes 2359296 | tf_op jit(solution)/shard_map/pallas_call | solution.py:355
  48.6 1.2 %shard_map.131.refs_3_ = f32[2,2,32,128]{3,2,1,0:T(8,128)S(1)} custom-call(s32[6]{0:T(128)S(1)} %copy-done.10, s32[6]{0:T(128)S(1)} %copy-done.15, f32[8,6,64,128]{3,2,1,0:T(8,128)S(1)} %get-tuple-element.12.gp_ref, f32[8,6,32,128]{3,2,1,0:T(8,128)S(1)} %get-tuple-element.11.cv_ref), custom_call_target="tpu_custom_call" | custom-call | flops 6291456 | bytes 2359296 | tf_op jit(solution)/shard_map/pallas_call | solution.py:355
  49.9 1.0 shard_map.127.bk_ref
  50.9 3.0 %shard_map.132 = f32[8,104,128]{2,1,0:T(8,128)S(1)} custom-call(s32[6]{0:T(128)S(1)} %copy-done.11, s32[6]{0:T(128)S(1)} %copy-done.15, f32[2,1152]{1,0:T(2,128)S(1)} %add.35.st_ref, f32[8,128]{1,0:T(8,128)S(1)} %bitcast.14, f32[8,128]{1,0:T(8,128)S(1)} %bitcast.17, f32[8,6,64,128]{3,2,1,0:T(8,128)S(1)} %get-tuple-element.12.gp_ref, ...), custom_call_target="tpu_custom_call" | custom-call | flops 25165824 | bytes 3425280 | tf_op jit(solution)/shard_map/pallas_call | solution.py:355
  53.9 0.7 copy-done.3
  54.6 4.1 %all-to-all-start.1 = ((f32[8,104,128]{2,1,0:T(8,128)}), f32[8,104,128]{2,1,0:T(8,128)S(1)}, u32[]{:S(2)}, u32[]{:S(2)}) async-start(f32[8,104,128]{2,1,0:T(8,128)} %copy-done.3), calls=%async_computation.1 | async-start | bytes 851968 | tf_op jit(solution)/shard_map/all_to_all | solution.py:454
  58.8 2.1 %shard_map.123 = bf16[4,128,128]{2,1,0:T(8,128)(2,1)S(1)} custom-call(s32[2]{0:T(128)S(1)} %pad_add_fusion.at_ref, bf16[8,192,128]{2,1,0:T(8,128)(2,1)S(1)} %all-to-all-done.recv_ref, bf16[192,1024]{1,0:T(8,128)(2,1)S(1)} %bitcast.11, bf16[192,1024]{1,0:T(8,128)(2,1)S(1)} %collective-permute-done.5.refs_1_, ...), custom_call_target="tpu_custom_call" | custom-call | flops 201326592 | bytes 3538944 | tf_op jit(solution)/shard_map/pallas_call | solution.py:355
  60.9 1.6 %collective-permute-start.12 = (bf16[4,128,128]{2,1,0:T(8,128)(2,1)S(1)}, bf16[4,128,128]{2,1,0:T(8,128)(2,1)S(1)}, u32[]{:S(2)}, u32[]{:S(2)}) collective-permute-start(bf16[4,128,128]{2,1,0:T(8,128)(2,1)S(1)} %shard_map.123), channel_id=1, source_target_pairs={{0,1},{1,0},{2,3},{3,2},{4,5},{5,4},{6,7},{7,6},{8,9},{9,8},{10,11... | collective-permute-start | bytes 393224 | tf_op jit(solution)/shard_map/ppermute | solution.py:384
  62.5 4.8 %all-to-all-done.1.recv_ref = f32[8,104,128]{2,1,0:T(8,128)S(1)} async-done(((f32[8,104,128]{2,1,0:T(8,128)}), f32[8,104,128]{2,1,0:T(8,128)S(1)}, u32[]{:S(2)}, u32[]{:S(2)}) %all-to-all-start.1) | async-done | bytes 426016 | tf_op jit(solution)/shard_map/all_to_all | solution.py:454
  67.4 1.6 %collective-permute-start.15 = (f32[104,128]{1,0:T(8,128)S(1)}, f32[104,128]{1,0:T(8,128)S(1)}, u32[]{:S(2)}, u32[]{:S(2)}) collective-permute-start(f32[104,128]{1,0:T(8,128)S(1)} %shard_map.133), channel_id=1, source_target_pairs={{0,1},{1,0},{2,3},{3,2},{4,5},{5,4},{6,7},{7,6},{8,9},{9,8},{10,11... | collective-permute-start | bytes 159752 | tf_op jit(solution)/shard_map/ppermute | solution.py:384
  69.0 2.1 %shard_map.122.own_ref = bf16[4,128,128]{2,1,0:T(8,128)(2,1)S(1)} custom-call(s32[2]{0:T(128)S(1)} %pad_add_fusion.at_ref, bf16[8,192,128]{2,1,0:T(8,128)(2,1)S(1)} %all-to-all-done.recv_ref, bf16[192,1024]{1,0:T(8,128)(2,1)S(1)} %bitcast.12, bf16[192,1024]{1,0:T(8,128)(2,1)S(1)} %collective-permute-done.5.refs_1_, ...), custom_call_target="tpu_custom_call" | custom-call | flops 201326592 | bytes 3538944 | tf_op jit(solution)/shard_map/pallas_call | solution.py:355
  71.2 2.7 %collective-permute-start.13 = (bf16[4,128,128]{2,1,0:T(8,128)(2,1)S(1)}, bf16[4,128,128]{2,1,0:T(8,128)(2,1)S(1)}, u32[]{:S(2)}, u32[]{:S(2)}) collective-permute-start(bf16[4,128,128]{2,1,0:T(8,128)(2,1)S(1)} %shard_map.124.own_ref), channel_id=1, source_target_pairs={{0,2},{1,3},{2,0},{3,1},{4,6},{5,7},{6,4},{7,5},{8,10},{9,11},{10,... | collective-permute-start | bytes 393224 | tf_op jit(solution)/shard_map/ppermute | solution.py:384
  73.9 0.9 collective-permute-start.16
  74.8 5.6 %collective-permute-done.16.recv_ref = f32[104,128]{1,0:T(8,128)S(1)} collective-permute-done((f32[104,128]{1,0:T(8,128)S(1)}, f32[104,128]{1,0:T(8,128)S(1)}, u32[]{:S(2)}, u32[]{:S(2)}) %collective-permute-start.16) | collective-permute-done | bytes 53280 | tf_op jit(solution)/shard_map/ppermute | solution.py:384
  80.5 1.2 %shard_map.134 = (f32[32,128]{1,0:T(8,128)}, f32[2,1024]{1,0:T(2,128)S(1)}) custom-call(s32[2]{0:T(128)S(1)} %pad_add_fusion.at_ref, f32[104,128]{1,0:T(8,128)S(1)} %add.37.own_ref, f32[104,128]{1,0:T(8,128)S(1)} %collective-permute-done.16.recv_ref, f32[2,1152]{1,0:T(2,128)S(1)} %add.35.st_ref, f32[8,128]{1,0:T(8,128)S(1)} %bitcast.15), custom_call_target="tpu_custom_call" | custom-call | bytes 119808 | tf_op jit(solution)/shard_map/pallas_call | solution.py:355
  81.6 2.1 %collective-permute-start.17 = (f32[2,1024]{1,0:T(2,128)S(1)}, f32[2,1024]{1,0:T(2,128)S(1)}, u32[]{:S(2)}, u32[]{:S(2)}) collective-permute-start(f32[2,1024]{1,0:T(2,128)S(1)} %get-tuple-element.14), channel_id=1, source_target_pairs={{0,12},{1,13},{2,14},{3,15},{4,8},{5,9},{6,10},{7,11},{8,4},{9,5},... | collective-permute-start | bytes 24584 | tf_op jit(solution)/shard_map/ppermute | solution.py:384
  83.8 1.4 %collective-permute-done.17 = f32[2,1024]{1,0:T(2,128)S(1)} collective-permute-done((f32[2,1024]{1,0:T(2,128)S(1)}, f32[2,1024]{1,0:T(2,128)S(1)}, u32[]{:S(2)}, u32[]{:S(2)}) %collective-permute-start.17) | collective-permute-done | bytes 8224 | tf_op jit(solution)/shard_map/ppermute | solution.py:384
  85.6 2.6 %collective-permute-done.18 = f32[2,1024]{1,0:T(2,128)S(1)} collective-permute-done((f32[2,1024]{1,0:T(2,128)S(1)}, f32[2,1024]{1,0:T(2,128)S(1)}, u32[]{:S(2)}, u32[]{:S(2)}) %collective-permute-start.18) | collective-permute-done | bytes 8224 | tf_op jit(solution)/shard_map/ppermute | solution.py:384
  88.2 0.5 collective-permute-start.19
  88.7 2.7 %shard_map.121 = bf16[6,32,1024]{2,1,0:T(8,128)(2,1)} custom-call(bf16[8,192,128]{2,1,0:T(8,128)(2,1)} %shard_map.120.hid_ref, bf16[1024,1024]{1,0:T(8,128)(2,1)S(1)} %copy-done.1), custom_call_target="tpu_custom_call" | custom-call | bytes 2490368 | tf_op jit(solution)/shard_map/pallas_call | solution.py:355
  91.5 0.6 fusion
  92.2 4.8 %collective-permute-done.14.recv_ref = bf16[4,128,128]{2,1,0:T(8,128)(2,1)S(1)} collective-permute-done((bf16[4,128,128]{2,1,0:T(8,128)(2,1)S(1)}, bf16[4,128,128]{2,1,0:T(8,128)(2,1)S(1)}, u32[]{:S(2)}, u32[]{:S(2)}) %collective-permute-start.14) | collective-permute-done | bytes 131104 | tf_op jit(solution)/shard_map/ppermute | solution.py:384
  97.0 1.4 %shard_map.126 = f32[128,1024]{1,0:T(8,128)} custom-call(s32[2]{0:T(128)S(1)} %pad_add_fusion.at_ref, bf16[4,128,128]{2,1,0:T(8,128)(2,1)S(1)} %shard_map.125.own_ref, bf16[4,128,128]{2,1,0:T(8,128)(2,1)S(1)} %collective-permute-done.14.recv_ref), custom_call_target="tpu_custom_call" | custom-call | bytes 262144 | tf_op jit(solution)/shard_map/pallas_call | solution.py:355
  (59 shorter events, 2.6 us)
Async XLA Ops:
  0.6 42.5 %copy-start.2 = (bf16[6,32,1024]{2,1,0:T(8,128)(2,1)S(1)}, bf16[6,32,1024]{2,1,0:T(8,128)(2,1)}, u32[]{:S(2)}) copy-start(bf16[6,32,1024]{2,1,0:T(8,128)(2,1)} %param.9) | copy-start | bytes 1179652
  0.6 12.4 %collective-permute-start.5 = (bf16[192,1024]{1,0:T(8,128)(2,1)}, bf16[192,1024]{1,0:T(8,128)(2,1)S(1)}, u32[]{:S(2)}, u32[]{:S(2)}) collective-permute-start(bf16[192,1024]{1,0:T(8,128)(2,1)} %bitcast.7), channel_id=1, source_target_pairs={{0,8},{1,9},{2,10},{3,11},{4,12},{5,13},{6,14},{7,15},{8,0},{9,1},... | collective-permute-start | bytes 1179656 | tf_op jit(solution)/shard_map/ppermute | solution.py:384
  3.7 40.0 %collective-permute-start.6 = (bf16[192,1024]{1,0:T(8,128)(2,1)}, bf16[192,1024]{1,0:T(8,128)(2,1)}, u32[]{:S(2)}, u32[]{:S(2)}) collective-permute-start(bf16[192,1024]{1,0:T(8,128)(2,1)} %bitcast.8), channel_id=1, source_target_pairs={{0,16},{1,17},{2,18},{3,19},{4,20},{5,21},{6,22},{7,23},{8,24},{9,... | collective-permute-start | bytes 1179656 | tf_op jit(solution)/shard_map/ppermute | solution.py:384
  13.0 31.1 %collective-permute-start.7 = (bf16[192,1024]{1,0:T(8,128)(2,1)S(1)}, bf16[192,1024]{1,0:T(8,128)(2,1)}, u32[]{:S(2)}, u32[]{:S(2)}) collective-permute-start(bf16[192,1024]{1,0:T(8,128)(2,1)S(1)} %collective-permute-done.5.refs_1_), channel_id=1, source_target_pairs={{0,16},{1,17},{2,18},{3,19},{4,20},{5,21},{6,22},{7,23},{8,24},{9,... | collective-permute-start | bytes 1179656 | tf_op jit(solution)/shard_map/ppermute | solution.py:384
  14.8 1.1 %copy-start.4 = (bf16[6,32,2048]{2,1,0:T(8,128)(2,1)S(1)}, bf16[6,32,2048]{2,1,0:T(8,128)(2,1)}, u32[]{:S(2)}) copy-start(bf16[6,32,2048]{2,1,0:T(8,128)(2,1)} %acts_ref.1) | copy-start | bytes 2359300
  15.9 0.9 copy-start.5
  16.8 0.7 copy-start.8
  17.5 0.7 copy-start.12
  18.1 26.1 %copy-start.10 = (s32[6]{0:T(128)S(1)}, s32[6]{0:T(128)}, u32[]{:S(2)}) copy-start(s32[6]{0:T(128)} %len_ref.13) | copy-start | bytes 76
  20.7 3.2 %collective-permute-start = (f32[2,1152]{1,0:T(2,128)S(1)}, f32[2,1152]{1,0:T(2,128)S(1)}, u32[]{:S(2)}, u32[]{:S(2)}) collective-permute-start(f32[2,1152]{1,0:T(2,128)S(1)} %get-tuple-element.10), channel_id=1, source_target_pairs={{0,5},{1,4},{2,7},{3,6},{4,1},{5,0},{6,3},{7,2},{8,13},{9,12},{10,... | collective-permute-start | bytes 27656 | tf_op jit(solution)/shard_map/ppermute | solution.py:384
  23.9 4.0 %collective-permute-start.1 = (f32[2,1152]{1,0:T(2,128)S(1)}, f32[2,1152]{1,0:T(2,128)S(1)}, u32[]{:S(2)}, u32[]{:S(2)}) collective-permute-start(f32[2,1152]{1,0:T(2,128)S(1)} %add.31), channel_id=1, source_target_pairs={{0,6},{1,7},{2,4},{3,5},{4,2},{5,3},{6,0},{7,1},{8,14},{9,15},{10,... | collective-permute-start | bytes 27656 | tf_op jit(solution)/shard_map/ppermute | solution.py:384
  27.9 3.1 %collective-permute-start.2 = (f32[2,1152]{1,0:T(2,128)S(1)}, f32[2,1152]{1,0:T(2,128)S(1)}, u32[]{:S(2)}, u32[]{:S(2)}) collective-permute-start(f32[2,1152]{1,0:T(2,128)S(1)} %add.32), channel_id=1, source_target_pairs={{0,12},{1,13},{2,14},{3,15},{4,8},{5,9},{6,10},{7,11},{8,4},{9,5},... | collective-permute-start | bytes 27656 | tf_op jit(solution)/shard_map/ppermute | solution.py:384
  31.0 3.1 %collective-permute-start.3 = (f32[2,1152]{1,0:T(2,128)S(1)}, f32[2,1152]{1,0:T(2,128)S(1)}, u32[]{:S(2)}, u32[]{:S(2)}) collective-permute-start(f32[2,1152]{1,0:T(2,128)S(1)} %add.33), channel_id=1, source_target_pairs={{0,20},{1,21},{2,22},{3,23},{4,16},{5,17},{6,18},{7,19},{8,28},{9,... | collective-permute-start | bytes 27656 | tf_op jit(solution)/shard_map/ppermute | solution.py:384
  34.1 1.2 %collective-permute-start.4 = (f32[2,1152]{1,0:T(2,128)S(1)}, f32[2,1152]{1,0:T(2,128)S(1)}, u32[]{:S(2)}, u32[]{:S(2)}) collective-permute-start(f32[2,1152]{1,0:T(2,128)S(1)} %add.34), channel_id=1, source_target_pairs={{0,4},{1,5},{2,6},{3,7},{4,0},{5,1},{6,2},{7,3},{8,12},{9,13},{10,... | collective-permute-start | bytes 27656 | tf_op jit(solution)/shard_map/ppermute | solution.py:384
  35.3 0.7 copy-start.6
  35.9 0.7 copy-start.9
  36.6 0.7 copy-start.13
  37.3 0.7 copy-start.16
  39.7 15.0 %all-to-all-start = ((bf16[8,192,128]{2,1,0:T(8,128)(2,1)}), bf16[8,192,128]{2,1,0:T(8,128)(2,1)S(1)}, u32[]{:S(2)}, u32[]{:S(2)}) async-start(bf16[8,192,128]{2,1,0:T(8,128)(2,1)} %shard_map.120.hid_ref), calls=%async_computation | async-start | bytes 786432 | tf_op jit(solution)/shard_map/all_to_all | solution.py:445
  43.1 15.6 %collective-permute-start.8 = (bf16[192,1024]{1,0:T(8,128)(2,1)S(1)}, bf16[192,1024]{1,0:T(8,128)(2,1)}, u32[]{:S(2)}, u32[]{:S(2)}) collective-permute-start(bf16[192,1024]{1,0:T(8,128)(2,1)S(1)} %bitcast.9), channel_id=1, source_target_pairs={{0,4},{1,5},{2,6},{3,7},{4,0},{5,1},{6,2},{7,3},{8,12},{9,13},{10,... | collective-permute-start | bytes 1179656 | tf_op jit(solution)/shard_map/ppermute | solution.py:384
  43.5 15.2 %collective-permute-start.9 = (bf16[192,1024]{1,0:T(8,128)(2,1)S(1)}, bf16[192,1024]{1,0:T(8,128)(2,1)}, u32[]{:S(2)}, u32[]{:S(2)}) collective-permute-start(bf16[192,1024]{1,0:T(8,128)(2,1)S(1)} %collective-permute-done.5.refs_1_), channel_id=1, source_target_pairs={{0,4},{1,5},{2,6},{3,7},{4,0},{5,1},{6,2},{7,3},{8,12},{9,13},{10,... | collective-permute-start | bytes 1179656 | tf_op jit(solution)/shard_map/ppermute | solution.py:384
  43.7 15.1 %collective-permute-start.10 = (bf16[192,1024]{1,0:T(8,128)(2,1)}, bf16[192,1024]{1,0:T(8,128)(2,1)}, u32[]{:S(2)}, u32[]{:S(2)}) collective-permute-start(bf16[192,1024]{1,0:T(8,128)(2,1)} %collective-permute-done.6.refs_2_), channel_id=1, source_target_pairs={{0,4},{1,5},{2,6},{3,7},{4,0},{5,1},{6,2},{7,3},{8,12},{9,13},{10,... | collective-permute-start | bytes 1179656 | tf_op jit(solution)/shard_map/ppermute | solution.py:384
  44.1 14.7 %collective-permute-start.11 = (bf16[192,1024]{1,0:T(8,128)(2,1)}, bf16[192,1024]{1,0:T(8,128)(2,1)}, u32[]{:S(2)}, u32[]{:S(2)}) collective-permute-start(bf16[192,1024]{1,0:T(8,128)(2,1)} %collective-permute-done.7.refs_3_), channel_id=1, source_target_pairs={{0,4},{1,5},{2,6},{3,7},{4,0},{5,1},{6,2},{7,3},{8,12},{9,13},{10,... | collective-permute-start | bytes 1179656 | tf_op jit(solution)/shard_map/ppermute | solution.py:384
  44.2 0.7 copy-start.14
  44.9 2.5 %copy-start.15 = (s32[6]{0:T(128)S(1)}, s32[6]{0:T(128)}, u32[]{:S(2)}) copy-start(s32[6]{0:T(128)} %off_ref.13) | copy-start | bytes 76
  47.4 2.5 %copy-start = (bf16[1024,1024]{1,0:T(8,128)(2,1)S(1)}, bf16[1024,1024]{1,0:T(8,128)(2,1)}, u32[]{:S(2)}) copy-start(bf16[1024,1024]{1,0:T(8,128)(2,1)} %w_ref.3) | copy-start | bytes 6291460
  49.9 1.0 %copy-start.7 = (f32[1024]{0:T(1024)S(1)}, f32[1024]{0:T(1024)}, u32[]{:S(2)}) copy-start(f32[1024]{0:T(1024)} %param.13) | copy-start | bytes 12292
  49.9 1.0 %copy-start.11 = (s32[6]{0:T(128)S(1)}, s32[6]{0:T(128)}, u32[]{:S(2)}) copy-start(s32[6]{0:T(128)} %len_ref.13) | copy-start | bytes 76
  49.9 1.0 %copy-start.17 = (f32[1024]{0:T(1024)S(1)}, f32[1024]{0:T(1024)}, u32[]{:S(2)}) copy-start(f32[1024]{0:T(1024)} %param.14) | copy-start | bytes 12292
  53.9 0.8 copy-start.3
  54.6 12.7 %all-to-all-start.1 = ((f32[8,104,128]{2,1,0:T(8,128)}), f32[8,104,128]{2,1,0:T(8,128)S(1)}, u32[]{:S(2)}, u32[]{:S(2)}) async-start(f32[8,104,128]{2,1,0:T(8,128)} %copy-done.3), calls=%async_computation.1 | async-start | bytes 851968 | tf_op jit(solution)/shard_map/all_to_all | solution.py:454
  60.9 10.2 %collective-permute-start.12 = (bf16[4,128,128]{2,1,0:T(8,128)(2,1)S(1)}, bf16[4,128,128]{2,1,0:T(8,128)(2,1)S(1)}, u32[]{:S(2)}, u32[]{:S(2)}) collective-permute-start(bf16[4,128,128]{2,1,0:T(8,128)(2,1)S(1)} %shard_map.123), channel_id=1, source_target_pairs={{0,1},{1,0},{2,3},{3,2},{4,5},{5,4},{6,7},{7,6},{8,9},{9,8},{10,11... | collective-permute-start | bytes 393224 | tf_op jit(solution)/shard_map/ppermute | solution.py:384
  67.4 21.3 %copy-start.1 = (bf16[1024,1024]{1,0:T(8,128)(2,1)S(1)}, bf16[1024,1024]{1,0:T(8,128)(2,1)}, u32[]{:S(2)}) copy-start(bf16[1024,1024]{1,0:T(8,128)(2,1)} %w_ref.3) | copy-start | bytes 6291460
  67.4 6.5 %collective-permute-start.15 = (f32[104,128]{1,0:T(8,128)S(1)}, f32[104,128]{1,0:T(8,128)S(1)}, u32[]{:S(2)}, u32[]{:S(2)}) collective-permute-start(f32[104,128]{1,0:T(8,128)S(1)} %shard_map.133), channel_id=1, source_target_pairs={{0,1},{1,0},{2,3},{3,2},{4,5},{5,4},{6,7},{7,6},{8,9},{9,8},{10,11... | collective-permute-start | bytes 159752 | tf_op jit(solution)/shard_map/ppermute | solution.py:384
  71.2 20.2 %collective-permute-start.13 = (bf16[4,128,128]{2,1,0:T(8,128)(2,1)S(1)}, bf16[4,128,128]{2,1,0:T(8,128)(2,1)S(1)}, u32[]{:S(2)}, u32[]{:S(2)}) collective-permute-start(bf16[4,128,128]{2,1,0:T(8,128)(2,1)S(1)} %shard_map.124.own_ref), channel_id=1, source_target_pairs={{0,2},{1,3},{2,0},{3,1},{4,6},{5,7},{6,4},{7,5},{8,10},{9,11},{10,... | collective-permute-start | bytes 393224 | tf_op jit(solution)/shard_map/ppermute | solution.py:384
  73.9 6.6 %collective-permute-start.16 = (f32[104,128]{1,0:T(8,128)S(1)}, f32[104,128]{1,0:T(8,128)S(1)}, u32[]{:S(2)}, u32[]{:S(2)}) collective-permute-start(f32[104,128]{1,0:T(8,128)S(1)} %add.37.own_ref), channel_id=1, source_target_pairs={{0,2},{1,3},{2,0},{3,1},{4,6},{5,7},{6,4},{7,5},{8,10},{9,11},{10,... | collective-permute-start | bytes 159752 | tf_op jit(solution)/shard_map/ppermute | solution.py:384
  81.6 3.5 %collective-permute-start.17 = (f32[2,1024]{1,0:T(2,128)S(1)}, f32[2,1024]{1,0:T(2,128)S(1)}, u32[]{:S(2)}, u32[]{:S(2)}) collective-permute-start(f32[2,1024]{1,0:T(2,128)S(1)} %get-tuple-element.14), channel_id=1, source_target_pairs={{0,12},{1,13},{2,14},{3,15},{4,8},{5,9},{6,10},{7,11},{8,4},{9,5},... | collective-permute-start | bytes 24584 | tf_op jit(solution)/shard_map/ppermute | solution.py:384
  85.1 3.1 %collective-permute-start.18 = (f32[2,1024]{1,0:T(2,128)S(1)}, f32[2,1024]{1,0:T(2,128)S(1)}, u32[]{:S(2)}, u32[]{:S(2)}) collective-permute-start(f32[2,1024]{1,0:T(2,128)S(1)} %add.38), channel_id=1, source_target_pairs={{0,20},{1,21},{2,22},{3,23},{4,16},{5,17},{6,18},{7,19},{8,28},{9,... | collective-permute-start | bytes 24584 | tf_op jit(solution)/shard_map/ppermute | solution.py:384
  88.2 3.2 %collective-permute-start.19 = (f32[2,1024]{1,0:T(2,128)S(1)}, f32[2,1024]{1,0:T(2,128)S(1)}, u32[]{:S(2)}, u32[]{:S(2)}) collective-permute-start(f32[2,1024]{1,0:T(2,128)S(1)} %add.39), channel_id=1, source_target_pairs={{0,4},{1,5},{2,6},{3,7},{4,0},{5,1},{6,2},{7,3},{8,12},{9,13},{10,... | collective-permute-start | bytes 24584 | tf_op jit(solution)/shard_map/ppermute | solution.py:384
  91.5 5.5 %collective-permute-start.14 = (bf16[4,128,128]{2,1,0:T(8,128)(2,1)S(1)}, bf16[4,128,128]{2,1,0:T(8,128)(2,1)S(1)}, u32[]{:S(2)}, u32[]{:S(2)}) collective-permute-start(bf16[4,128,128]{2,1,0:T(8,128)(2,1)S(1)} %shard_map.125.own_ref), channel_id=1, source_target_pairs={{0,1},{1,0},{2,3},{3,2},{4,5},{5,4},{6,7},{7,6},{8,9},{9,8},{10,11... | collective-permute-start | bytes 393224 | tf_op jit(solution)/shard_map/ppermute | solution.py:384

commit v2 on v1

--- a/solution.py
+++ b/solution.py
@@ -95,12 +95,6 @@
     return (outputs, weight_rows, kernel_rows.T, gamma_sum, beta_sum)
 
 
-def mask_of(len_ref, off_ref, slot, frames):
-    length, offset = len_ref[slot], off_ref[slot]
-    position = lax.broadcasted_iota(jnp.int32, (frames, LANES), 0)
-    return ((position >= offset) & (position < offset + length)).astype(F32)
-
-
 def fold(value):
     total = value[0:8]
     for at in range(8, value.shape[0], 8):
@@ -112,18 +106,27 @@
     return jnp.sum(value, axis=0, keepdims=True)
 
 
-def conv_body(len_ref, off_ref, acts_ref, k_ref, gp_ref, cv_ref, st_ref, acc_ref):
+def conv_body(len_ref, off_ref, acts_ref, k_ref, gp_ref, cv_ref, st_ref, ok_ref, in_ref, acc_ref):
     _, frames, wide = acts_ref.shape
     blocks, slots, rows, _ = gp_ref.shape
     taps = k_ref.shape[0]
     lead = taps // 2
     slot = pl.program_id(0)
+    low = off_ref[slot]
+    high = low + len_ref[slot]
 
     @pl.when(slot == 0)
     def _():
         acc_ref[...] = jnp.zeros_like(acc_ref)
 
-    valid = mask_of(len_ref, off_ref, slot, frames)
+    position = lax.broadcasted_iota(jnp.int32, (frames, LANES), 0)
+    valid = ((position >= low) & (position < high)).astype(F32)
+    ok_ref[slot] = valid
+    at = lax.broadcasted_iota(jnp.int32, (taps, frames), 1)
+    at = at - lax.broadcasted_iota(jnp.int32, (taps, frames), 0) + (lead - 1)
+    in_ref[slot] = (
+        (at >= low) & (at < high) & (at >= 0) & (at < frames)
+    ).astype(F32)
     for block in range(blocks):
         cols = slice(block * LANES, (block + 1) * LANES)
         gate = slice(wide // 2 + block * LANES, wide // 2 + (block + 1) * LANES)
@@ -135,7 +138,8 @@
         cols = slice(block * LANES, (block + 1) * LANES)
         total = gp_ref[block, slot, 1 : 1 + frames, :] * k_ref[0:1, cols]
         for tap in range(1, taps):
-            total = total + gp_ref[block, slot, 1 + tap : 1 + tap + frames, :] * k_ref[tap : tap + 1, cols]
+            lag = gp_ref[block, slot, 1 + tap : 1 + tap + frames, :]
+            total = total + lag * k_ref[tap : tap + 1, cols]
         cv_ref[block, slot] = total
         masked = total * valid
         acc_ref[0, block] += fold(masked)
@@ -168,17 +172,15 @@
             put(low + j, row_sum(sums[j]))
 
 
-def aux_body(start, len_ref, off_ref, gp_ref, cv_ref, out_ref, wt_ref):
+def aux_body(start, ok_ref, in_ref, gp_ref, cv_ref, out_ref, wt_ref):
     _, slots, frames, _ = cv_ref.shape
     many, _, taps, _ = out_ref.shape
     lead = taps // 2
-    lag = lax.broadcasted_iota(jnp.int32, (taps, frames), 0)
-    at = lax.broadcasted_iota(jnp.int32, (taps, frames), 1) - lag + (lead - 1)
 
     def one(i, carry):
         block = start + i
         for slot in range(slots):
-            wt_ref[slot] = cv_ref[block, slot] * mask_of(len_ref, off_ref, slot, frames)
+            wt_ref[slot] = cv_ref[block, slot] * ok_ref[slot]
 
         def put(k, row):
             out_ref[i, 0, k : k + 1, :] = row
@@ -186,12 +188,7 @@
         lag_sums(gp_ref, block, lambda slot: wt_ref[slot], taps, 16, put)
         total = jnp.zeros((taps, LANES), F32)
         for slot in range(slots):
-            inside = (
-                (at >= off_ref[slot])
-                & (at < off_ref[slot] + len_ref[slot])
-                & (at >= 0)
-                & (at < frames)
-            ).astype(BF16)
+            inside = in_ref[slot].astype(BF16)
             rest = gp_ref[block, slot, lead : lead + frames, :]
             for _ in range(3):
                 part = rest.astype(BF16)
@@ -220,14 +217,14 @@
     return count, mean, inv
 
 
-def hidden_body(len_ref, off_ref, st_ref, g_ref, b_ref, cv_ref, hid_ref):
+def hidden_body(st_ref, g_ref, b_ref, ok_ref, cv_ref, hid_ref):
     blocks, slots, frames, _ = cv_ref.shape
 
     def one(block, carry):
         _, mean, inv = scale_of(st_ref, block)
         gain, shift = g_ref[pl.ds(block, 1), :], b_ref[pl.ds(block, 1), :]
         for slot in range(slots):
-            valid = mask_of(len_ref, off_ref, slot, frames)
+            valid = ok_ref[slot]
             shifted = gain * ((cv_ref[block, slot] - mean) * inv) + shift
             hidden = shifted * jax.nn.sigmoid(shifted) * valid
             hid_ref[block, slot * frames : (slot + 1) * frames, :] = hidden.astype(BF16)
@@ -236,23 +233,23 @@
     lax.fori_loop(0, blocks, one, 0)
 
 
-def slope_body(len_ref, off_ref, st_ref, g_ref, b_ref, gp_ref, cv_ref, bk_ref, *refs):
+def slope_body(st_ref, g_ref, b_ref, ok_ref, gp_ref, cv_ref, bk_ref, *refs):
     aux_refs, q_ref, sl_ref = refs[:-2], refs[-2], refs[-1]
-    _, slots, frames, _ = cv_ref.shape
+    blocks, slots, frames, _ = cv_ref.shape
     taps = aux_refs[0].shape[2]
     each = aux_refs[0].shape[0]
+    last = 3 * taps
 
     def one(block, aux_ref, i):
         _, mean, inv = scale_of(st_ref, block)
         gain, shift = g_ref[pl.ds(block, 1), :], b_ref[pl.ds(block, 1), :]
         first = second = jnp.zeros((8, LANES), F32)
         for slot in range(slots):
-            valid = mask_of(len_ref, off_ref, slot, frames)
             normed = (cv_ref[block, slot] - mean) * inv
             shifted = gain * normed + shift
             sig = jax.nn.sigmoid(shifted)
             back = bk_ref[block, slot * frames : (slot + 1) * frames, :]
-            slope = back * sig * (1.0 + shifted * (1.0 - sig)) * valid
+            slope = back * sig * (1.0 + shifted * (1.0 - sig)) * ok_ref[slot]
             sl_ref[slot] = slope
             first, second = first + fold(slope), second + fold(slope * normed)
 
@@ -261,11 +258,9 @@
 
         lag_sums(gp_ref, block, lambda slot: sl_ref[slot], taps, 16, put)
         q_ref[block, taps : 2 * taps, :] = aux_ref[i, 1]
-        q_ref[block, 2 * taps : 3 * taps, :] = inv * (aux_ref[i, 0] - mean * aux_ref[i, 1])
-        q_ref[block, 3 * taps : 3 * taps + 1, :] = row_sum(first)
-        q_ref[block, 3 * taps + 1 : 3 * taps + 2, :] = row_sum(second)
-        left = q_ref.shape[1] - 3 * taps - 2
-        q_ref[block, 3 * taps + 2 :, :] = jnp.zeros((left, LANES), F32)
+        q_ref[block, 2 * taps : last, :] = inv * (aux_ref[i, 0] - mean * aux_ref[i, 1])
+        q_ref[0, pl.ds(last + block, 1), :] = row_sum(first)
+        q_ref[0, pl.ds(last + blocks + block, 1), :] = row_sum(second)
 
     for part, aux_ref in enumerate(aux_refs):
 
@@ -274,6 +269,8 @@
             return carry
 
         lax.fori_loop(0, each, step, 0)
+    for block in range(1, blocks):
+        q_ref[block, last:, :] = q_ref[0, last:, :]
 
 
 def out_body(hid_ref, w_ref, out_ref):
@@ -308,41 +305,53 @@
         out_ref[block] = total[:, block * LANES : (block + 1) * LANES].astype(BF16)
 
 
-def add_body(own_ref, recv_ref, out_ref):
-    out_ref[...] = (own_ref[...].astype(F32) + recv_ref[...].astype(F32)).astype(out_ref.dtype)
-
-
-def sum_body(recv_ref, out_ref):
-    total = recv_ref[0]
-    for source in range(1, recv_ref.shape[0]):
-        total = total + recv_ref[source]
-    out_ref[...] = total
-
-
-def last_body(taps, at_ref, own_ref, recv_ref, st_ref, g_ref, gk_ref, gs_ref):
-    me = at_ref[0]
-    value = own_ref[...] + recv_ref[...]
-    count, _, inv = scale_of(st_ref, me)
-    beta_sum = value[3 * taps : 3 * taps + 1]
-    gamma_sum = value[3 * taps + 1 : 3 * taps + 2]
-    gk_ref[...] = (g_ref[pl.ds(me, 1), :] * inv) * (
-        value[0:taps]
-        - (beta_sum / count) * value[taps : 2 * taps]
-        - (gamma_sum / count) * value[2 * taps : 3 * taps]
-    )
-    gs_ref[...] = jnp.zeros_like(gs_ref)
-    cols = pl.ds(pl.multiple_of(me * LANES, LANES), LANES)
-    gs_ref[0:1, cols] = gamma_sum
-    gs_ref[1:2, cols] = beta_sum
-
-
-def spread_body(at_ref, own_ref, recv_ref, out_ref):
-    half = at_ref[1]
+def put_pair(ref, at, value):
+    rows = value.shape[0]
+    lead = value.astype(BF16)
+    ref[at : at + rows, :] = lead
+    ref[at + rows : at + 2 * rows, :] = (value - lead.astype(F32)).astype(BF16)
+
+
+def get_pair(ref, at, rows):
+    return ref[at : at + rows, :].astype(F32) + ref[at + rows : at + 2 * rows, :].astype(F32)
+
+
+def join_body(own_ref, recv_ref, lags_ref, out_ref):
     many = own_ref.shape[0]
+    for block in range(many):
+        rows = slice(block * LANES, (block + 1) * LANES)
+        out_ref[rows, :] = (own_ref[block].astype(F32) + recv_ref[block].astype(F32)).astype(BF16)
+    total = lags_ref[0]
+    for source in range(1, lags_ref.shape[0]):
+        total = total + lags_ref[source]
+    put_pair(out_ref, many * LANES, total)
+
+
+def add_body(n_w, own_ref, recv_ref, out_ref):
+    n_q = (own_ref.shape[0] - n_w) // 2
+    out_ref[0:n_w, :] = (own_ref[0:n_w, :].astype(F32) + recv_ref[0:n_w, :].astype(F32)).astype(BF16)
+    put_pair(out_ref, n_w, get_pair(own_ref, n_w, n_q) + get_pair(recv_ref, n_w, n_q))
+
+
+def last_body(n_w, taps, at_ref, own_ref, recv_ref, st_ref, g_ref, rows_ref, gk_ref, gg_ref, gb_ref):
+    me, half = at_ref[0], at_ref[1]
+    many = n_w // LANES
     for which, ref in ((half, own_ref), (1 - half, recv_ref)):
         for block in range(many):
             cols = pl.ds(pl.multiple_of((which * many + block) * LANES, LANES), LANES)
-            out_ref[:, cols] = ref[block].astype(F32)
+            rows_ref[:, cols] = ref[block * LANES : (block + 1) * LANES, :].astype(F32)
+    n_q = (own_ref.shape[0] - n_w) // 2
+    value = get_pair(own_ref, n_w, n_q) + get_pair(recv_ref, n_w, n_q)
+    blocks = g_ref.shape[0]
+    gb_ref[...] = value[3 * taps : 3 * taps + blocks]
+    gg_ref[...] = value[3 * taps + blocks : 3 * taps + 2 * blocks]
+    count, _, inv = scale_of(st_ref, me)
+    mine = pl.ds(me, 1)
+    gk_ref[...] = (g_ref[mine, :] * inv) * (
+        value[0:taps]
+        - (gb_ref[mine, :] / count) * value[taps : 2 * taps]
+        - (gg_ref[mine, :] / count) * value[2 * taps : 3 * taps]
+    )
 
 
 SMEM = pl.BlockSpec(memory_space=pltpu.SMEM)
@@ -370,7 +379,7 @@
     taps = kernel.shape[0]
     blocks = width // LANES
     tokens = slots * frames
-    n_q = 3 * taps + 8
+    n_q = 3 * taps + 2 * blocks
     padded = 2 * (taps // 2) + frames
     me_dp, me_grp = lax.axis_index("dp"), lax.axis_index("grp")
     shape = jax.ShapeDtypeStruct
@@ -394,12 +403,14 @@
         pieces += [(m | bit, swap(v, bit, 0)) for m, v in pieces]
     masks, values = tuple(m for m, _ in pieces), [v for _, v in pieces]
 
-    gated, conv_out, stats = call(
+    gated, conv_out, stats, valid, inside = call(
         conv_body,
         [
             shape((blocks, slots, padded, LANES), F32),
             shape((blocks, slots, frames, LANES), F32),
             shape((2, width + LANES), F32),
+            shape((slots, frames, LANES), F32),
+            shape((slots, taps, frames), F32),
         ],
         (lengths, offsets),
         (acts, kernel),
@@ -421,15 +432,13 @@
         flops=2 * tokens * width * width,
     )
     parts = 4
-    while blocks % parts:
-        parts //= 2
     each = blocks // parts
     aux = [
         call(
             functools.partial(aux_body, i * each),
             shape((each, 2, taps, LANES), F32),
-            (lengths, offsets),
-            (gated, conv_out),
+            (),
+            (valid, inside, gated, conv_out),
             flops=4 * taps * tokens * each * LANES,
             scratch=[pltpu.VMEM((slots, frames, LANES), F32)],
         )
@@ -439,15 +448,15 @@
     hidden = call(
         hidden_body,
         shape((blocks, tokens, LANES), BF16),
-        (lengths, offsets),
-        (stats, gamma2, beta2, conv_out),
+        (),
+        (stats, gamma2, beta2, valid, conv_out),
     )
     received = lax.all_to_all(hidden, "dp", 0, 0, tiled=True)
     lags = call(
         slope_body,
         shape((blocks, n_q, LANES), F32),
-        (lengths, offsets),
-        (stats, gamma2, beta2, gated, conv_out, back, *aux),
+        (),
+        (stats, gamma2, beta2, valid, gated, conv_out, back, *aux),
         flops=4 * taps * tokens * width,
         scratch=[pltpu.VMEM((slots, frames, LANES), F32)],
     )
@@ -456,6 +465,7 @@
 
     half_shape = shape((blocks // 2, LANES, LANES), BF16)
     flops = n_dp * tokens * LANES * width
+    n_w = blocks // 2 * LANES
 
     def rows_of(flip):
         body = functools.partial(rows_body, masks, flip)
@@ -464,24 +474,24 @@
     given = rows_of(True)
     taken = swap(given, 0, 1)
     kept = rows_of(False)
-    both = call(add_body, half_shape, (), (kept, taken))
+    both_shape = shape((n_w + 2 * n_q, LANES), BF16)
+    both = call(join_body, both_shape, (), (kept, taken, lags))
     for mask in grp_bits[1:]:
-        both = call(add_body, half_shape, (), (both, swap(both, 0, mask)))
+        other = swap(both, 0, mask)
+        both = call(functools.partial(add_body, n_w), both_shape, (), (both, other))
     rest = swap(both, 0, 1)
-
-    lags = call(sum_body, shape((n_q, LANES), F32), (), (lags,))
-    for mask in grp_bits[:-1]:
-        lags = lags + swap(lags, 0, mask)
-    grad_kernel, small = call(
-        functools.partial(last_body, taps),
-        [shape((taps, LANES), F32), shape((2, width), F32)],
+    weight_rows, grad_kernel, gamma_sum, beta_sum = call(
+        functools.partial(last_body, n_w, taps),
+        [
+            shape((LANES, width), F32),
+            shape((taps, LANES), F32),
+            shape((blocks, LANES), F32),
+            shape((blocks, LANES), F32),
+        ],
         (at,),
-        (lags, swap(lags, 0, grp_bits[-1]), stats, gamma2),
-    )
-    for mask in dp_bits[1:] + [0]:
-        small = small + swap(small, mask | 1, 0)
-    weight_rows = call(spread_body, shape((LANES, width), F32), (at,), (both, rest))
-    return (outputs, weight_rows, grad_kernel, small[0], small[1])
+        (both, rest, stats, gamma2),
+    )
+    return (outputs, weight_rows, grad_kernel, gamma_sum.reshape(width), beta_sum.reshape(width))
 
 
 def solution(mesh):
@@ -496,6 +506,7 @@
             and width == n_dp * LANES
             and taps % 16 == 0
             and frames % 16 == 0
+            and n_dp % 8 == 0
         )
 
     def local(acts, cotan, lengths, offsets, kernel, gamma, beta, w_out):

time: 98.9 us -> 82.8 us (0.84)
  waiting for transfers between devices: 37.4 us -> 31.6 us
  starting transfers between devices: 29.1 us -> 24 us
  Pallas kernels: 22.7 us -> 20 us
  local copies, waits for them, and re-layouts: 8.08 us -> 5.73 us
    ppermute x20 -> x15, starting transfers between devices: 21.6 us -> 16.5 us  [swap(): return lax.ppermute(value, ('dp', 'grp'), pairs)]
    ppermute x20 -> x15, waiting for transfers between devices: 32.6 us -> 29.3 us  [swap(): return lax.ppermute(value, ('dp', 'grp'), pairs)]
    pallas_call x16 -> x14, Pallas kernels: 22.7 us -> 20 us  [call(): pl.pallas_call(body, in_specs=more.pop('in_specs', None) or [SMEM] * len(...]
    all_to_all x1, waiting for transfers between devices: 4.82 us -> 2.26 us  [local_fast(): lags = lax.all_to_all(lags, 'dp', 0, 0, tiled=True)]
    unnamed x36 -> x22, local copies, waits for them, and re-layouts: 7.47 us -> 5.73 us
  transfers between devices with their start and end apart: 22 -> 17, of which waited for: 11 -> 11; matrix products, arithmetic and copies ran while one was open for 1% -> 0% of each run, Pallas kernels for 22% -> 21%
where the time goes in v2:
time: 82.8 us; the launch traced here: 82.2 us
  waiting for transfers between devices  31.6 us (38%)
  starting transfers between devices  24 us (29%)
  Pallas kernels  20 us (24%)
  local copies, waits for them, and re-layouts  5.73 us (7%)
    ppermute x15, waiting for transfers between devices, swap(): return lax.ppermute(value, ('dp', 'grp'), pairs)  29.3 us
    pallas_call x14, Pallas kernels, call(): pl.pallas_call(body, in_specs=more.pop('in_specs', None) or [SMEM] * len(...  20 us
    ppermute x15, starting transfers between devices, swap(): return lax.ppermute(value, ('dp', 'grp'), pairs)  16.5 us
    unnamed x22, local copies, waits for them, and re-layouts  5.73 us
    all_to_all x1, starting transfers between devices, local_fast(): lags = lax.all_to_all(lags, 'dp', 0, 0, tiled=True)  3.99 us
    all_to_all x1, starting transfers between devices, local_fast(): received = lax.all_to_all(hidden, 'dp', 0, 0, tiled=True)  3.45 us
    all_to_all x1, waiting for transfers between devices, local_fast(): lags = lax.all_to_all(lags, 'dp', 0, 0, tiled=True)  2.26 us
  transfers between devices with their start and end apart: 17, of which 11 were waited for; matrix products, arithmetic and copies ran while one was open for 0% of the time, Pallas kernels for 21%

profile of v2, /device:TPU:0, one launch (start us, length us, event | category | flops | bytes accessed | tf_op | source)
XLA Modules:
  0.0 82.2 jit_solution(6174615205113705888)
XLA Ops:
  0.6 3.0 %collective-permute-start.5 = (bf16[192,1024]{1,0:T(8,128)(2,1)}, bf16[192,1024]{1,0:T(8,128)(2,1)}, u32[]{:S(2)}, u32[]{:S(2)}) collective-permute-start(bf16[192,1024]{1,0:T(8,128)(2,1)} %bitcast.7), channel_id=1, source_target_pairs={{0,8},{1,9},{2,10},{3,11},{4,12},{5,13},{6,14},{7,15},{8,0},{9,1},... | collective-permute-start | bytes 1179656 | tf_op jit(solution)/shard_map/ppermute | solution.py:393
  3.7 1.5 %collective-permute-start.6 = (bf16[192,1024]{1,0:T(8,128)(2,1)}, bf16[192,1024]{1,0:T(8,128)(2,1)}, u32[]{:S(2)}, u32[]{:S(2)}) collective-permute-start(bf16[192,1024]{1,0:T(8,128)(2,1)} %bitcast.8), channel_id=1, source_target_pairs={{0,16},{1,17},{2,18},{3,19},{4,20},{5,21},{6,22},{7,23},{8,24},{9,... | collective-permute-start | bytes 1179656 | tf_op jit(solution)/shard_map/ppermute | solution.py:393
  5.2 7.9 %collective-permute-done.5.refs_1_ = bf16[192,1024]{1,0:T(8,128)(2,1)} collective-permute-done((bf16[192,1024]{1,0:T(8,128)(2,1)}, bf16[192,1024]{1,0:T(8,128)(2,1)}, u32[]{:S(2)}, u32[]{:S(2)}) %collective-permute-start.5) | collective-permute-done | bytes 393248 | tf_op jit(solution)/shard_map/ppermute | solution.py:393
  13.1 1.8 %collective-permute-start.7 = (bf16[192,1024]{1,0:T(8,128)(2,1)}, bf16[192,1024]{1,0:T(8,128)(2,1)}, u32[]{:S(2)}, u32[]{:S(2)}) collective-permute-start(bf16[192,1024]{1,0:T(8,128)(2,1)} %collective-permute-done.5.refs_1_), channel_id=1, source_target_pairs={{0,16},{1,17},{2,18},{3,19},{4,20},{5,21},{6,22},{7,23},{8,24},{9,... | collective-permute-start | bytes 1179656 | tf_op jit(solution)/shard_map/ppermute | solution.py:393
  14.9 1.1 %copy-done.4 = bf16[6,32,2048]{2,1,0:T(8,128)(2,1)S(1)} copy-done((bf16[6,32,2048]{2,1,0:T(8,128)(2,1)S(1)}, bf16[6,32,2048]{2,1,0:T(8,128)(2,1)}, u32[]{:S(2)}) %copy-start.4) | copy-done | bytes 786456
  16.0 0.9 %copy-done.5 = f32[32,1024]{1,0:T(8,128)S(1)} copy-done((f32[32,1024]{1,0:T(8,128)S(1)}, f32[32,1024]{1,0:T(8,128)}, u32[]{:S(2)}) %copy-start.5) | copy-done | bytes 131096
  16.9 0.7 copy-done.9
  17.6 0.7 copy-done.10
  18.2 2.6 %shard_map.119 = (f32[8,6,64,128]{3,2,1,0:T(8,128)S(1)}, f32[8,6,32,128]{3,2,1,0:T(8,128)S(1)}, f32[2,1152]{1,0:T(2,128)S(1)}, f32[6,32,128]{2,1,0:T(8,128)S(1)}, f32[6,32,32]{2,1,0:T(8,128)S(1)}) custom-call(s32[6]{0:T(128)S(1)} %copy-done.9, s32[6]{0:T(128)S(1)} %copy-done.10, bf16[6,32,2048]{2,1,0:T(8,128)(2,1)S(1)} %copy-done.4, f32[32,1024]{1,0:T(8,128)S(1)} %copy-done.5), custom_call_target="tpu_custom_call" | custom-call | flops 25165824 | bytes 917504 | tf_op jit(solution)/shard_map/pallas_call | solution.py:364
  20.9 3.1 %collective-permute-done = f32[2,1152]{1,0:T(2,128)S(1)} collective-permute-done((f32[2,1152]{1,0:T(2,128)S(1)}, f32[2,1152]{1,0:T(2,128)S(1)}, u32[]{:S(2)}, u32[]{:S(2)}) %collective-permute-start) | collective-permute-done | bytes 9248 | tf_op jit(solution)/shard_map/ppermute | solution.py:393
  24.0 2.3 %collective-permute-start.1 = (f32[2,1152]{1,0:T(2,128)S(1)}, f32[2,1152]{1,0:T(2,128)S(1)}, u32[]{:S(2)}, u32[]{:S(2)}) collective-permute-start(f32[2,1152]{1,0:T(2,128)S(1)} %add.19), channel_id=1, source_target_pairs={{0,6},{1,7},{2,4},{3,5},{4,2},{5,3},{6,0},{7,1},{8,14},{9,15},{10,... | collective-permute-start | bytes 27656 | tf_op jit(solution)/shard_map/ppermute | solution.py:393
  26.3 1.7 %collective-permute-done.1 = f32[2,1152]{1,0:T(2,128)S(1)} collective-permute-done((f32[2,1152]{1,0:T(2,128)S(1)}, f32[2,1152]{1,0:T(2,128)S(1)}, u32[]{:S(2)}, u32[]{:S(2)}) %collective-permute-start.1) | collective-permute-done | bytes 9248 | tf_op jit(solution)/shard_map/ppermute | solution.py:393
  28.0 1.2 %collective-permute-start.2 = (f32[2,1152]{1,0:T(2,128)S(1)}, f32[2,1152]{1,0:T(2,128)S(1)}, u32[]{:S(2)}, u32[]{:S(2)}) collective-permute-start(f32[2,1152]{1,0:T(2,128)S(1)} %add.20), channel_id=1, source_target_pairs={{0,12},{1,13},{2,14},{3,15},{4,8},{5,9},{6,10},{7,11},{8,4},{9,5},... | collective-permute-start | bytes 27656 | tf_op jit(solution)/shard_map/ppermute | solution.py:393
  29.2 1.9 %collective-permute-done.2 = f32[2,1152]{1,0:T(2,128)S(1)} collective-permute-done((f32[2,1152]{1,0:T(2,128)S(1)}, f32[2,1152]{1,0:T(2,128)S(1)}, u32[]{:S(2)}, u32[]{:S(2)}) %collective-permute-start.2) | collective-permute-done | bytes 9248 | tf_op jit(solution)/shard_map/ppermute | solution.py:393
  31.1 0.5 collective-permute-start.3
  31.6 2.6 %collective-permute-done.3 = f32[2,1152]{1,0:T(2,128)S(1)} collective-permute-done((f32[2,1152]{1,0:T(2,128)S(1)}, f32[2,1152]{1,0:T(2,128)S(1)}, u32[]{:S(2)}, u32[]{:S(2)}) %collective-permute-start.3) | collective-permute-done | bytes 9248 | tf_op jit(solution)/shard_map/ppermute | solution.py:393
  34.2 0.1 collective-permute-start.4
  34.3 1.1 %collective-permute-done.4 = f32[2,1152]{1,0:T(2,128)S(1)} collective-permute-done((f32[2,1152]{1,0:T(2,128)S(1)}, f32[2,1152]{1,0:T(2,128)S(1)}, u32[]{:S(2)}, u32[]{:S(2)}) %collective-permute-start.4) | collective-permute-done | bytes 9248 | tf_op jit(solution)/shard_map/ppermute | solution.py:393
  35.4 0.7 copy-done.6
  36.1 0.7 copy-done.8
  36.8 1.2 %shard_map.120.hid_ref = bf16[8,192,128]{2,1,0:T(8,128)(2,1)} custom-call(f32[2,1152]{1,0:T(2,128)S(1)} %add.23.st_ref, f32[8,128]{1,0:T(8,128)S(1)} %bitcast.13, f32[8,128]{1,0:T(8,128)S(1)} %bitcast.16, f32[6,32,128]{2,1,0:T(8,128)S(1)} %get-tuple-element.15.ok_ref, f32[8,6,32,128]{3,2,1,0:T(8,128)S(1)} %get-tuple-element.16.cv_ref), custom_call_target="tpu_custom_call" | custom-call | bytes 902144 | tf_op jit(solution)/shard_map/pallas_call | solution.py:364
  37.9 3.5 %all-to-all-start = ((bf16[8,192,128]{2,1,0:T(8,128)(2,1)}), bf16[8,192,128]{2,1,0:T(8,128)(2,1)S(1)}, u32[]{:S(2)}, u32[]{:S(2)}) async-start(bf16[8,192,128]{2,1,0:T(8,128)(2,1)} %shard_map.120.hid_ref), calls=%async_computation | async-start | bytes 786432 | tf_op jit(solution)/shard_map/all_to_all | solution.py:454
  41.4 0.4 collective-permute-start.8
  41.8 0.2 collective-permute-start.9
  42.0 0.3 collective-permute-start.10
  42.3 0.2 collective-permute-start.11
  42.5 0.7 shard_map.128.refs_3_
  43.2 0.7 shard_map.127.refs_2_
  43.8 0.7 shard_map.126.refs_1_
  44.5 0.7 shard_map.125.refs_0_
  45.2 0.2 copy-done
  45.4 1.0 %shard_map.124.bk_ref = f32[8,192,128]{2,1,0:T(8,128)S(1)} custom-call(bf16[192,1024]{1,0:T(8,128)(2,1)S(1)} %bitcast.10, bf16[1024,1024]{1,0:T(8,128)(2,1)S(1)} %copy-done), custom_call_target="tpu_custom_call" | custom-call | flops 402653184 | bytes 2490368 | tf_op jit(solution)/shard_map/pallas_call | solution.py:364
  46.4 2.4 %shard_map.129 = f32[8,112,128]{2,1,0:T(8,128)S(1)} custom-call(f32[2,1152]{1,0:T(2,128)S(1)} %add.23.st_ref, f32[8,128]{1,0:T(8,128)S(1)} %bitcast.14, f32[8,128]{1,0:T(8,128)S(1)} %bitcast.17, f32[6,32,128]{2,1,0:T(8,128)S(1)} %get-tuple-element.15.ok_ref, f32[8,6,64,128]{3,2,1,0:T(8,128)S(1)} %get-tuple-element.17.gp_ref, ...), custom_call_target="tpu_custom_call" | custom-call | flops 25165824 | bytes 3523584 | tf_op jit(solution)/shard_map/pallas_call | solution.py:364
  48.8 0.8 copy-done.3
  49.6 4.0 %all-to-all-start.1 = ((f32[8,112,128]{2,1,0:T(8,128)}), f32[8,112,128]{2,1,0:T(8,128)S(1)}, u32[]{:S(2)}, u32[]{:S(2)}) async-start(f32[8,112,128]{2,1,0:T(8,128)} %copy-done.3), calls=%async_computation.1 | async-start | bytes 917504 | tf_op jit(solution)/shard_map/all_to_all | solution.py:463
  53.6 0.1 pad_add_fusion.at_ref
  53.7 2.9 %shard_map.123 = bf16[4,128,128]{2,1,0:T(8,128)(2,1)} custom-call(s32[2]{0:T(128)S(1)} %pad_add_fusion.at_ref, bf16[8,192,128]{2,1,0:T(8,128)(2,1)S(1)} %all-to-all-done.recv_ref, bf16[192,1024]{1,0:T(8,128)(2,1)S(1)} %bitcast.11, bf16[192,1024]{1,0:T(8,128)(2,1)} %collective-permute-done.5.refs_1_, bf16[192,1024]{1,0:T(8,128)(2,1)} %collective-permute-done.6.refs_2_, ...), custom_call_target="tpu_custom_call" | custom-call | flops 201326592 | bytes 3538944 | tf_op jit(solution)/shard_map/pallas_call | solution.py:364
  56.6 1.6 %collective-permute-start.12 = (bf16[4,128,128]{2,1,0:T(8,128)(2,1)}, bf16[4,128,128]{2,1,0:T(8,128)(2,1)}, u32[]{:S(2)}, u32[]{:S(2)}) collective-permute-start(bf16[4,128,128]{2,1,0:T(8,128)(2,1)} %shard_map.123), channel_id=1, source_target_pairs={{0,1},{1,0},{2,3},{3,2},{4,5},{5,4},{6,7},{7,6},{8,9},{9,8},{10,11... | collective-permute-start | bytes 393224 | tf_op jit(solution)/shard_map/ppermute | solution.py:393
  58.2 2.2 %shard_map.122.own_ref = bf16[4,128,128]{2,1,0:T(8,128)(2,1)S(1)} custom-call(s32[2]{0:T(128)S(1)} %pad_add_fusion.at_ref, bf16[8,192,128]{2,1,0:T(8,128)(2,1)S(1)} %all-to-all-done.recv_ref, bf16[192,1024]{1,0:T(8,128)(2,1)S(1)} %bitcast.12, bf16[192,1024]{1,0:T(8,128)(2,1)} %collective-permute-done.5.refs_1_, ...), custom_call_target="tpu_custom_call" | custom-call | flops 201326592 | bytes 3538944 | tf_op jit(solution)/shard_map/pallas_call | solution.py:364
  60.4 2.3 %all-to-all-done.1.lags_ref = f32[8,112,128]{2,1,0:T(8,128)S(1)} async-done(((f32[8,112,128]{2,1,0:T(8,128)}), f32[8,112,128]{2,1,0:T(8,128)S(1)}, u32[]{:S(2)}, u32[]{:S(2)}) %all-to-all-start.1) | async-done | bytes 458784 | tf_op jit(solution)/shard_map/all_to_all | solution.py:463
  62.6 0.2 collective-permute-done.12.recv_ref
  62.8 1.0 %shard_map.130.own_ref = bf16[736,128]{1,0:T(8,128)(2,1)S(1)} custom-call(bf16[4,128,128]{2,1,0:T(8,128)(2,1)S(1)} %shard_map.122.own_ref, bf16[4,128,128]{2,1,0:T(8,128)(2,1)} %collective-permute-done.12.recv_ref, f32[8,112,128]{2,1,0:T(8,128)S(1)} %all-to-all-done.1.lags_ref), custom_call_target="tpu_custom_call" | custom-call | bytes 720896 | tf_op jit(solution)/shard_map/pallas_call | solution.py:364
  63.8 2.7 %collective-permute-start.13 = (bf16[736,128]{1,0:T(8,128)(2,1)S(1)}, bf16[736,128]{1,0:T(8,128)(2,1)S(1)}, u32[]{:S(2)}, u32[]{:S(2)}) collective-permute-start(bf16[736,128]{1,0:T(8,128)(2,1)S(1)} %shard_map.130.own_ref), channel_id=1, source_target_pairs={{0,2},{1,3},{2,0},{3,1},{4,6},{5,7},{6,4},{7,5},{8,10},{9,11},{10,... | collective-permute-start | bytes 565256 | tf_op jit(solution)/shard_map/ppermute | solution.py:393
  66.4 8.6 %collective-permute-done.13.recv_ref = bf16[736,128]{1,0:T(8,128)(2,1)S(1)} collective-permute-done((bf16[736,128]{1,0:T(8,128)(2,1)S(1)}, bf16[736,128]{1,0:T(8,128)(2,1)S(1)}, u32[]{:S(2)}, u32[]{:S(2)}) %collective-permute-start.13) | collective-permute-done | bytes 188448 | tf_op jit(solution)/shard_map/ppermute | solution.py:393
  75.1 0.7 collective-permute-start.14
  75.8 2.7 %shard_map.121 = bf16[6,32,1024]{2,1,0:T(8,128)(2,1)} custom-call(bf16[8,192,128]{2,1,0:T(8,128)(2,1)} %shard_map.120.hid_ref, bf16[1024,1024]{1,0:T(8,128)(2,1)S(1)} %copy-done.1), custom_call_target="tpu_custom_call" | custom-call | bytes 2490368 | tf_op jit(solution)/shard_map/pallas_call | solution.py:364
  78.5 2.2 %collective-permute-done.14.recv_ref = bf16[736,128]{1,0:T(8,128)(2,1)S(1)} collective-permute-done((bf16[736,128]{1,0:T(8,128)(2,1)S(1)}, bf16[736,128]{1,0:T(8,128)(2,1)S(1)}, u32[]{:S(2)}, u32[]{:S(2)}) %collective-permute-start.14) | collective-permute-done | bytes 188448 | tf_op jit(solution)/shard_map/ppermute | solution.py:393
  80.8 1.4 %shard_map.132 = (f32[128,1024]{1,0:T(8,128)}, f32[32,128]{1,0:T(8,128)}, f32[8,128]{1,0:T(8,128)}, f32[8,128]{1,0:T(8,128)}) custom-call(s32[2]{0:T(128)S(1)} %pad_add_fusion.at_ref, bf16[736,128]{1,0:T(8,128)(2,1)S(1)} %shard_map.131.own_ref, bf16[736,128]{1,0:T(8,128)(2,1)S(1)} %collective-permute-done.14.recv_ref, f32[2,1152]{1,0:T(2,128)S(1)} %add.23.st_ref, ...), custom_call_target="tpu_custom_call" | custom-call | bytes 390144 | tf_op jit(solution)/shard_map/pallas_call | solution.py:364
  (28 shorter events, 0.3 us)
Async XLA Ops:
  0.6 40.7 %copy-start.2 = (bf16[6,32,1024]{2,1,0:T(8,128)(2,1)S(1)}, bf16[6,32,1024]{2,1,0:T(8,128)(2,1)}, u32[]{:S(2)}) copy-start(bf16[6,32,1024]{2,1,0:T(8,128)(2,1)} %param.9) | copy-start | bytes 1179652
  0.6 12.5 %collective-permute-start.5 = (bf16[192,1024]{1,0:T(8,128)(2,1)}, bf16[192,1024]{1,0:T(8,128)(2,1)}, u32[]{:S(2)}, u32[]{:S(2)}) collective-permute-start(bf16[192,1024]{1,0:T(8,128)(2,1)} %bitcast.7), channel_id=1, source_target_pairs={{0,8},{1,9},{2,10},{3,11},{4,12},{5,13},{6,14},{7,15},{8,0},{9,1},... | collective-permute-start | bytes 1179656 | tf_op jit(solution)/shard_map/ppermute | solution.py:393
  3.7 38.3 %collective-permute-start.6 = (bf16[192,1024]{1,0:T(8,128)(2,1)}, bf16[192,1024]{1,0:T(8,128)(2,1)}, u32[]{:S(2)}, u32[]{:S(2)}) collective-permute-start(bf16[192,1024]{1,0:T(8,128)(2,1)} %bitcast.8), channel_id=1, source_target_pairs={{0,16},{1,17},{2,18},{3,19},{4,20},{5,21},{6,22},{7,23},{8,24},{9,... | collective-permute-start | bytes 1179656 | tf_op jit(solution)/shard_map/ppermute | solution.py:393
  13.1 29.2 %collective-permute-start.7 = (bf16[192,1024]{1,0:T(8,128)(2,1)}, bf16[192,1024]{1,0:T(8,128)(2,1)}, u32[]{:S(2)}, u32[]{:S(2)}) collective-permute-start(bf16[192,1024]{1,0:T(8,128)(2,1)} %collective-permute-done.5.refs_1_), channel_id=1, source_target_pairs={{0,16},{1,17},{2,18},{3,19},{4,20},{5,21},{6,22},{7,23},{8,24},{9,... | collective-permute-start | bytes 1179656 | tf_op jit(solution)/shard_map/ppermute | solution.py:393
  14.9 1.1 %copy-start.4 = (bf16[6,32,2048]{2,1,0:T(8,128)(2,1)S(1)}, bf16[6,32,2048]{2,1,0:T(8,128)(2,1)}, u32[]{:S(2)}) copy-start(bf16[6,32,2048]{2,1,0:T(8,128)(2,1)} %acts_ref.1) | copy-start | bytes 2359300
  16.0 0.9 %copy-start.5 = (f32[32,1024]{1,0:T(8,128)S(1)}, f32[32,1024]{1,0:T(8,128)}, u32[]{:S(2)}) copy-start(f32[32,1024]{1,0:T(8,128)} %k_ref.1) | copy-start | bytes 393220
  16.9 0.7 copy-start.9
  17.6 0.7 copy-start.10
  20.9 3.2 %collective-permute-start = (f32[2,1152]{1,0:T(2,128)S(1)}, f32[2,1152]{1,0:T(2,128)S(1)}, u32[]{:S(2)}, u32[]{:S(2)}) collective-permute-start(f32[2,1152]{1,0:T(2,128)S(1)} %get-tuple-element.14), channel_id=1, source_target_pairs={{0,5},{1,4},{2,7},{3,6},{4,1},{5,0},{6,3},{7,2},{8,13},{9,12},{10,... | collective-permute-start | bytes 27656 | tf_op jit(solution)/shard_map/ppermute | solution.py:393
  24.0 4.0 %collective-permute-start.1 = (f32[2,1152]{1,0:T(2,128)S(1)}, f32[2,1152]{1,0:T(2,128)S(1)}, u32[]{:S(2)}, u32[]{:S(2)}) collective-permute-start(f32[2,1152]{1,0:T(2,128)S(1)} %add.19), channel_id=1, source_target_pairs={{0,6},{1,7},{2,4},{3,5},{4,2},{5,3},{6,0},{7,1},{8,14},{9,15},{10,... | collective-permute-start | bytes 27656 | tf_op jit(solution)/shard_map/ppermute | solution.py:393
  28.0 3.1 %collective-permute-start.2 = (f32[2,1152]{1,0:T(2,128)S(1)}, f32[2,1152]{1,0:T(2,128)S(1)}, u32[]{:S(2)}, u32[]{:S(2)}) collective-permute-start(f32[2,1152]{1,0:T(2,128)S(1)} %add.20), channel_id=1, source_target_pairs={{0,12},{1,13},{2,14},{3,15},{4,8},{5,9},{6,10},{7,11},{8,4},{9,5},... | collective-permute-start | bytes 27656 | tf_op jit(solution)/shard_map/ppermute | solution.py:393
  31.1 3.1 %collective-permute-start.3 = (f32[2,1152]{1,0:T(2,128)S(1)}, f32[2,1152]{1,0:T(2,128)S(1)}, u32[]{:S(2)}, u32[]{:S(2)}) collective-permute-start(f32[2,1152]{1,0:T(2,128)S(1)} %add.21), channel_id=1, source_target_pairs={{0,20},{1,21},{2,22},{3,23},{4,16},{5,17},{6,18},{7,19},{8,28},{9,... | collective-permute-start | bytes 27656 | tf_op jit(solution)/shard_map/ppermute | solution.py:393
  34.2 1.2 %collective-permute-start.4 = (f32[2,1152]{1,0:T(2,128)S(1)}, f32[2,1152]{1,0:T(2,128)S(1)}, u32[]{:S(2)}, u32[]{:S(2)}) collective-permute-start(f32[2,1152]{1,0:T(2,128)S(1)} %add.22), channel_id=1, source_target_pairs={{0,4},{1,5},{2,6},{3,7},{4,0},{5,1},{6,2},{7,3},{8,12},{9,13},{10,... | collective-permute-start | bytes 27656 | tf_op jit(solution)/shard_map/ppermute | solution.py:393
  35.4 0.7 copy-start.6
  36.1 0.7 copy-start.8
  37.9 11.7 %all-to-all-start = ((bf16[8,192,128]{2,1,0:T(8,128)(2,1)}), bf16[8,192,128]{2,1,0:T(8,128)(2,1)S(1)}, u32[]{:S(2)}, u32[]{:S(2)}) async-start(bf16[8,192,128]{2,1,0:T(8,128)(2,1)} %shard_map.120.hid_ref), calls=%async_computation | async-start | bytes 786432 | tf_op jit(solution)/shard_map/all_to_all | solution.py:454
  41.4 12.3 %collective-permute-start.8 = (bf16[192,1024]{1,0:T(8,128)(2,1)S(1)}, bf16[192,1024]{1,0:T(8,128)(2,1)}, u32[]{:S(2)}, u32[]{:S(2)}) collective-permute-start(bf16[192,1024]{1,0:T(8,128)(2,1)S(1)} %bitcast.9), channel_id=1, source_target_pairs={{0,4},{1,5},{2,6},{3,7},{4,0},{5,1},{6,2},{7,3},{8,12},{9,13},{10,... | collective-permute-start | bytes 1179656 | tf_op jit(solution)/shard_map/ppermute | solution.py:393
  41.8 11.9 %collective-permute-start.9 = (bf16[192,1024]{1,0:T(8,128)(2,1)}, bf16[192,1024]{1,0:T(8,128)(2,1)}, u32[]{:S(2)}, u32[]{:S(2)}) collective-permute-start(bf16[192,1024]{1,0:T(8,128)(2,1)} %collective-permute-done.5.refs_1_), channel_id=1, source_target_pairs={{0,4},{1,5},{2,6},{3,7},{4,0},{5,1},{6,2},{7,3},{8,12},{9,13},{10,... | collective-permute-start | bytes 1179656 | tf_op jit(solution)/shard_map/ppermute | solution.py:393
  42.0 11.7 %collective-permute-start.10 = (bf16[192,1024]{1,0:T(8,128)(2,1)}, bf16[192,1024]{1,0:T(8,128)(2,1)}, u32[]{:S(2)}, u32[]{:S(2)}) collective-permute-start(bf16[192,1024]{1,0:T(8,128)(2,1)} %collective-permute-done.6.refs_2_), channel_id=1, source_target_pairs={{0,4},{1,5},{2,6},{3,7},{4,0},{5,1},{6,2},{7,3},{8,12},{9,13},{10,... | collective-permute-start | bytes 1179656 | tf_op jit(solution)/shard_map/ppermute | solution.py:393
  42.3 11.4 %collective-permute-start.11 = (bf16[192,1024]{1,0:T(8,128)(2,1)}, bf16[192,1024]{1,0:T(8,128)(2,1)}, u32[]{:S(2)}, u32[]{:S(2)}) collective-permute-start(bf16[192,1024]{1,0:T(8,128)(2,1)} %collective-permute-done.7.refs_3_), channel_id=1, source_target_pairs={{0,4},{1,5},{2,6},{3,7},{4,0},{5,1},{6,2},{7,3},{8,12},{9,13},{10,... | collective-permute-start | bytes 1179656 | tf_op jit(solution)/shard_map/ppermute | solution.py:393
  43.8 1.6 %copy-start = (bf16[1024,1024]{1,0:T(8,128)(2,1)S(1)}, bf16[1024,1024]{1,0:T(8,128)(2,1)}, u32[]{:S(2)}) copy-start(bf16[1024,1024]{1,0:T(8,128)(2,1)} %w_ref.3) | copy-start | bytes 6291460
  45.4 1.0 %copy-start.7 = (f32[1024]{0:T(1024)S(1)}, f32[1024]{0:T(1024)}, u32[]{:S(2)}) copy-start(f32[1024]{0:T(1024)} %param.13) | copy-start | bytes 12292
  48.8 0.8 copy-start.3
  49.6 13.0 %all-to-all-start.1 = ((f32[8,112,128]{2,1,0:T(8,128)}), f32[8,112,128]{2,1,0:T(8,128)S(1)}, u32[]{:S(2)}, u32[]{:S(2)}) async-start(f32[8,112,128]{2,1,0:T(8,128)} %copy-done.3), calls=%async_computation.1 | async-start | bytes 917504 | tf_op jit(solution)/shard_map/all_to_all | solution.py:463
  56.6 19.3 %copy-start.1 = (bf16[1024,1024]{1,0:T(8,128)(2,1)S(1)}, bf16[1024,1024]{1,0:T(8,128)(2,1)}, u32[]{:S(2)}) copy-start(bf16[1024,1024]{1,0:T(8,128)(2,1)} %w_ref.3) | copy-start | bytes 6291460
  56.6 6.2 %collective-permute-start.12 = (bf16[4,128,128]{2,1,0:T(8,128)(2,1)}, bf16[4,128,128]{2,1,0:T(8,128)(2,1)}, u32[]{:S(2)}, u32[]{:S(2)}) collective-permute-start(bf16[4,128,128]{2,1,0:T(8,128)(2,1)} %shard_map.123), channel_id=1, source_target_pairs={{0,1},{1,0},{2,3},{3,2},{4,5},{5,4},{6,7},{7,6},{8,9},{9,8},{10,11... | collective-permute-start | bytes 393224 | tf_op jit(solution)/shard_map/ppermute | solution.py:393
  63.8 11.3 %collective-permute-start.13 = (bf16[736,128]{1,0:T(8,128)(2,1)S(1)}, bf16[736,128]{1,0:T(8,128)(2,1)S(1)}, u32[]{:S(2)}, u32[]{:S(2)}) collective-permute-start(bf16[736,128]{1,0:T(8,128)(2,1)S(1)} %shard_map.130.own_ref), channel_id=1, source_target_pairs={{0,2},{1,3},{2,0},{3,1},{4,6},{5,7},{6,4},{7,5},{8,10},{9,11},{10,... | collective-permute-start | bytes 565256 | tf_op jit(solution)/shard_map/ppermute | solution.py:393
  75.1 5.7 %collective-permute-start.14 = (bf16[736,128]{1,0:T(8,128)(2,1)S(1)}, bf16[736,128]{1,0:T(8,128)(2,1)S(1)}, u32[]{:S(2)}, u32[]{:S(2)}) collective-permute-start(bf16[736,128]{1,0:T(8,128)(2,1)S(1)} %shard_map.131.own_ref), channel_id=1, source_target_pairs={{0,1},{1,0},{2,3},{3,2},{4,5},{5,4},{6,7},{7,6},{8,9},{9,8},{10,11... | collective-permute-start | bytes 565256 | tf_op jit(solution)/shard_map/ppermute | solution.py:393

commit v3 on v2

--- a/solution.py
+++ b/solution.py
@@ -106,55 +106,71 @@
     return jnp.sum(value, axis=0, keepdims=True)
 
 
-def conv_body(len_ref, off_ref, acts_ref, k_ref, gp_ref, cv_ref, st_ref, ok_ref, in_ref, acc_ref):
-    _, frames, wide = acts_ref.shape
-    blocks, slots, rows, _ = gp_ref.shape
+def conv_body(len_hbm, off_hbm, acts_hbm, k_hbm, gp_ref, cv_ref, st_ref, ok_ref, in_ref,
+              acc_ref, len_ref, off_ref, acts_ref, k_ref, sems, slot_sems):
+    slots, frames, wide = acts_ref.shape
+    blocks, _, rows, _ = gp_ref.shape
     taps = k_ref.shape[0]
     lead = taps // 2
-    slot = pl.program_id(0)
-    low = off_ref[slot]
-    high = low + len_ref[slot]
-
-    @pl.when(slot == 0)
-    def _():
-        acc_ref[...] = jnp.zeros_like(acc_ref)
-
+    small = [
+        pltpu.make_async_copy(source, target, sems.at[i])
+        for i, (source, target) in enumerate(((len_hbm, len_ref), (off_hbm, off_ref), (k_hbm, k_ref)))
+    ]
+
+    def fetch(slot):
+        return pltpu.make_async_copy(acts_hbm.at[slot], acts_ref.at[slot], slot_sems.at[slot])
+
+    small[0].start()
+    small[1].start()
+    fetch(0).start()
+    small[2].start()
+    for slot in range(1, slots):
+        fetch(slot).start()
+    acc_ref[...] = jnp.zeros_like(acc_ref)
     position = lax.broadcasted_iota(jnp.int32, (frames, LANES), 0)
-    valid = ((position >= low) & (position < high)).astype(F32)
-    ok_ref[slot] = valid
-    at = lax.broadcasted_iota(jnp.int32, (taps, frames), 1)
-    at = at - lax.broadcasted_iota(jnp.int32, (taps, frames), 0) + (lead - 1)
-    in_ref[slot] = (
-        (at >= low) & (at < high) & (at >= 0) & (at < frames)
-    ).astype(F32)
+    reach = lax.broadcasted_iota(jnp.int32, (taps, frames), 1)
+    reach = reach - lax.broadcasted_iota(jnp.int32, (taps, frames), 0) + (lead - 1)
+    for copy in small:
+        copy.wait()
+
+    def one(slot, carry):
+        low = off_ref[slot]
+        high = low + len_ref[slot]
+        valid = ((position >= low) & (position < high)).astype(F32)
+        ok_ref[slot] = valid
+        in_ref[slot] = (
+            (reach >= low) & (reach < high) & (reach >= 0) & (reach < frames)
+        ).astype(F32)
+        fetch(slot).wait()
+        for block in range(blocks):
+            cols = slice(block * LANES, (block + 1) * LANES)
+            gate = slice(wide // 2 + block * LANES, wide // 2 + (block + 1) * LANES)
+            left, right = acts_ref[slot, :, cols].astype(F32), acts_ref[slot, :, gate].astype(F32)
+            gp_ref[block, slot, 0:lead, :] = jnp.zeros((lead, LANES), F32)
+            gp_ref[block, slot, lead : lead + frames, :] = left * jax.nn.sigmoid(right) * valid
+            tail = jnp.zeros((rows - lead - frames, LANES), F32)
+            gp_ref[block, slot, lead + frames : rows, :] = tail
+        for block in range(blocks):
+            cols = slice(block * LANES, (block + 1) * LANES)
+            total = gp_ref[block, slot, 1 : 1 + frames, :] * k_ref[0:1, cols]
+            for tap in range(1, taps):
+                lag = gp_ref[block, slot, 1 + tap : 1 + tap + frames, :]
+                total = total + lag * k_ref[tap : tap + 1, cols]
+            cv_ref[block, slot] = total
+            masked = total * valid
+            acc_ref[0, block] += fold(masked)
+            acc_ref[1, block] += fold(masked * total)
+        return carry
+
+    lax.fori_loop(0, slots, one, 0)
     for block in range(blocks):
         cols = slice(block * LANES, (block + 1) * LANES)
-        gate = slice(wide // 2 + block * LANES, wide // 2 + (block + 1) * LANES)
-        left, right = acts_ref[0, :, cols].astype(F32), acts_ref[0, :, gate].astype(F32)
-        gp_ref[block, slot, 0:lead, :] = jnp.zeros((lead, LANES), F32)
-        gp_ref[block, slot, lead : lead + frames, :] = left * jax.nn.sigmoid(right) * valid
-        gp_ref[block, slot, lead + frames : rows, :] = jnp.zeros((rows - lead - frames, LANES), F32)
-    for block in range(blocks):
-        cols = slice(block * LANES, (block + 1) * LANES)
-        total = gp_ref[block, slot, 1 : 1 + frames, :] * k_ref[0:1, cols]
-        for tap in range(1, taps):
-            lag = gp_ref[block, slot, 1 + tap : 1 + tap + frames, :]
-            total = total + lag * k_ref[tap : tap + 1, cols]
-        cv_ref[block, slot] = total
-        masked = total * valid
-        acc_ref[0, block] += fold(masked)
-        acc_ref[1, block] += fold(masked * total)
-
-    @pl.when(slot == slots - 1)
-    def _():
-        for block in range(blocks):
-            cols = slice(block * LANES, (block + 1) * LANES)
-            st_ref[0:1, cols] = row_sum(acc_ref[0, block])
-            st_ref[1:2, cols] = row_sum(acc_ref[1, block])
-        count = len_ref[0]
-        for other in range(1, slots):
-            count = count + len_ref[other]
-        st_ref[:, blocks * LANES :] = jnp.full((2, LANES), count.astype(F32), F32)
+        st_ref[0:1, cols] = row_sum(acc_ref[0, block])
+        st_ref[1:2, cols] = row_sum(acc_ref[1, block])
+    count = len_ref[0]
+    for other in range(1, slots):
+        count = count + len_ref[other]
+    st_ref[:, blocks * LANES :] = jnp.full((2, LANES), count.astype(F32), F32)
 
 
 def lag_sums(gp_ref, block, weights, taps, group, put):
@@ -200,14 +216,6 @@
     lax.fori_loop(0, many, one, 0)
 
 
-def back_body(cotan_ref, w_ref, out_ref):
-    for block in range(out_ref.shape[0]):
-        rows = w_ref[block * LANES : (block + 1) * LANES, :]
-        out_ref[block] = lax.dot_general(
-            cotan_ref[...], rows, (((1,), (1,)), ((), ())), preferred_element_type=F32
-        )
-
-
 def scale_of(st_ref, block):
     width = st_ref.shape[1] - LANES
     cols = pl.ds(pl.multiple_of(block * LANES, LANES), LANES)
@@ -233,7 +241,7 @@
     lax.fori_loop(0, blocks, one, 0)
 
 
-def slope_body(st_ref, g_ref, b_ref, ok_ref, gp_ref, cv_ref, bk_ref, *refs):
+def slope_body(st_ref, g_ref, b_ref, ok_ref, gp_ref, cv_ref, ct_ref, w_ref, *refs):
     aux_refs, q_ref, sl_ref = refs[:-2], refs[-2], refs[-1]
     blocks, slots, frames, _ = cv_ref.shape
     taps = aux_refs[0].shape[2]
@@ -243,12 +251,16 @@
     def one(block, aux_ref, i):
         _, mean, inv = scale_of(st_ref, block)
         gain, shift = g_ref[pl.ds(block, 1), :], b_ref[pl.ds(block, 1), :]
+        w_rows = w_ref[pl.ds(pl.multiple_of(block * LANES, LANES), LANES), :]
+        backs = lax.dot_general(
+            ct_ref[...], w_rows, (((1,), (1,)), ((), ())), preferred_element_type=F32
+        )
         first = second = jnp.zeros((8, LANES), F32)
         for slot in range(slots):
             normed = (cv_ref[block, slot] - mean) * inv
             shifted = gain * normed + shift
             sig = jax.nn.sigmoid(shifted)
-            back = bk_ref[block, slot * frames : (slot + 1) * frames, :]
+            back = backs[slot * frames : (slot + 1) * frames, :]
             slope = back * sig * (1.0 + shifted * (1.0 - sig)) * ok_ref[slot]
             sl_ref[slot] = slope
             first, second = first + fold(slope), second + fold(slope * normed)
@@ -289,16 +301,23 @@
 
 
 def rows_body(masks, flip, at_ref, recv_ref, *refs):
-    pieces, out_ref = refs[:-1], refs[-1]
+    pieces, (out_ref, held, sems) = refs[:-3], refs[-3:]
     me = at_ref[0]
     half = 1 - at_ref[1] if flip else at_ref[1]
-    width = pieces[0].shape[1] // 2
+    width = held.shape[2]
     cols = pl.ds(pl.multiple_of(half * width, width), width)
+    copies = [
+        pltpu.make_async_copy(piece.at[:, cols], held.at[i], sems.at[i])
+        for i, piece in enumerate(pieces)
+    ]
+    for copy in copies:
+        copy.start()
     total = None
-    for mask, piece in zip(masks, pieces):
+    for i, mask in enumerate(masks):
         left = recv_ref[jnp.bitwise_xor(me, mask)]
+        copies[i].wait()
         term = lax.dot_general(
-            left, piece[:, cols], (((0,), (0,)), ((), ())), preferred_element_type=F32
+            left, held[i], (((0,), (0,)), ((), ())), preferred_element_type=F32
         )
         total = term if total is None else total + term
     for block in range(width // LANES):
@@ -356,6 +375,12 @@
 
 SMEM = pl.BlockSpec(memory_space=pltpu.SMEM)
 VMEM = pl.BlockSpec(memory_space=pltpu.VMEM)
+HBM = pl.BlockSpec(memory_space=pltpu.HBM)
+ANY = pl.BlockSpec(memory_space=pl.ANY)
+
+
+def in_hbm(value):
+    return pltpu.with_memory_space_constraint(value, pltpu.HBM)
 
 
 def call(body, shapes, scalars, args, flops=0, scratch=(), mib=8, **more):
@@ -412,25 +437,25 @@
             shape((slots, frames, LANES), F32),
             shape((slots, taps, frames), F32),
         ],
-        (lengths, offsets),
-        (acts, kernel),
+        (),
+        [in_hbm(value) for value in (lengths, offsets, acts, kernel)],
         flops=4 * taps * tokens * width,
-        scratch=[pltpu.VMEM((2, blocks, 8, LANES), F32)],
-        grid=(slots,),
-        in_specs=[SMEM, SMEM, pl.BlockSpec((1, frames, wide), lambda s: (s, 0, 0)), VMEM],
+        scratch=[
+            pltpu.VMEM((2, blocks, 8, LANES), F32),
+            pltpu.SMEM((slots,), jnp.int32),
+            pltpu.SMEM((slots,), jnp.int32),
+            pltpu.VMEM(acts.shape, BF16),
+            pltpu.VMEM(kernel.shape, F32),
+            pltpu.SemaphoreType.DMA((3,)),
+            pltpu.SemaphoreType.DMA((slots,)),
+        ],
+        in_specs=[HBM] * 4,
     )
 
     hops = [(1, m) for m in grp_bits] + [(m | 1, 0) for m in dp_bits[1:]] + [(1, 0)]
     for dp_mask, grp_mask in hops:
         stats = stats + swap(stats, dp_mask, grp_mask)
 
-    back = call(
-        back_body,
-        shape((blocks, tokens, LANES), F32),
-        (),
-        (flat_cotan, w_out),
-        flops=2 * tokens * width * width,
-    )
     parts = 4
     each = blocks // parts
     aux = [
@@ -456,8 +481,8 @@
         slope_body,
         shape((blocks, n_q, LANES), F32),
         (),
-        (stats, gamma2, beta2, valid, gated, conv_out, back, *aux),
-        flops=4 * taps * tokens * width,
+        (stats, gamma2, beta2, valid, gated, conv_out, flat_cotan, w_out, *aux),
+        flops=4 * taps * tokens * width + 2 * tokens * width * width,
         scratch=[pltpu.VMEM((slots, frames, LANES), F32)],
     )
     lags = lax.all_to_all(lags, "dp", 0, 0, tiled=True)
@@ -469,7 +494,18 @@
 
     def rows_of(flip):
         body = functools.partial(rows_body, masks, flip)
-        return call(body, half_shape, (at,), (received, *values), flops=flops)
+        return call(
+            body,
+            half_shape,
+            (at,),
+            (received, *values),
+            flops=flops,
+            scratch=[
+                pltpu.VMEM((n_dp, tokens, width // 2), BF16),
+                pltpu.SemaphoreType.DMA((n_dp,)),
+            ],
+            in_specs=[SMEM, VMEM] + [ANY] * n_dp,
+        )
 
     given = rows_of(True)
     taken = swap(given, 0, 1)

time: 82.8 us -> 81.2 us (0.981)
  local copies, waits for them, and re-layouts: 5.73 us -> 2.37 us
  Pallas kernels: 20 us -> 22 us
  waiting for transfers between devices: 31.6 us -> 30.6 us
    unnamed x22 -> x14, local copies, waits for them, and re-layouts: 5.73 us -> 2.37 us
    pallas_call x14 -> x13, Pallas kernels: 20 us -> 22 us  [call(): pl.pallas_call(body, in_specs=more.pop('in_specs', None) or [SMEM] * len(...]
  transfers between devices with their start and end apart: 17 -> 17, of which waited for: 11 -> 10; matrix products, arithmetic and copies ran while one was open for 0% -> 0% of each run, Pallas kernels for 21% -> 24%
where the time goes in v3:
time: 81.2 us; the launch traced here: 80.7 us
  waiting for transfers between devices  30.6 us (38%)
  starting transfers between devices  24.8 us (31%)
  Pallas kernels  22 us (27%)
  local copies, waits for them, and re-layouts  2.37 us (3%)
    ppermute x15, waiting for transfers between devices, swap(): return lax.ppermute(value, ('dp', 'grp'), pairs)  28.9 us
    pallas_call x13, Pallas kernels, call(): pl.pallas_call(body, in_specs=more.pop('in_specs', None) or [SMEM] * len(...  22 us
    ppermute x15, starting transfers between devices, swap(): return lax.ppermute(value, ('dp', 'grp'), pairs)  17.3 us
    all_to_all x1, starting transfers between devices, local_fast(): lags = lax.all_to_all(lags, 'dp', 0, 0, tiled=True)  4.06 us
    all_to_all x1, starting transfers between devices, local_fast(): received = lax.all_to_all(hidden, 'dp', 0, 0, tiled=True)  3.45 us
    unnamed x14, local copies, waits for them, and re-layouts  2.37 us
    all_to_all x1, waiting for transfers between devices, local_fast(): lags = lax.all_to_all(lags, 'dp', 0, 0, tiled=True)  1.76 us
  transfers between devices with their start and end apart: 17, of which 10 were waited for; matrix products, arithmetic and copies ran while one was open for 0% of the time, Pallas kernels for 24%

profile of v3, /device:TPU:0, one launch (start us, length us, event | category | flops | bytes accessed | tf_op | source)
XLA Modules:
  0.0 80.7 jit_solution(15952872284019631370)
XLA Ops:
  0.6 3.0 %collective-permute-start.5 = (bf16[192,1024]{1,0:T(8,128)(2,1)}, bf16[192,1024]{1,0:T(8,128)(2,1)}, u32[]{:S(2)}, u32[]{:S(2)}) collective-permute-start(bf16[192,1024]{1,0:T(8,128)(2,1)} %bitcast.7), channel_id=1, source_target_pairs={{0,8},{1,9},{2,10},{3,11},{4,12},{5,13},{6,14},{7,15},{8,0},{9,1},... | collective-permute-start | bytes 1179656 | tf_op jit(solution)/shard_map/ppermute | solution.py:418
  3.7 1.5 %collective-permute-start.6 = (bf16[192,1024]{1,0:T(8,128)(2,1)}, bf16[192,1024]{1,0:T(8,128)(2,1)}, u32[]{:S(2)}, u32[]{:S(2)}) collective-permute-start(bf16[192,1024]{1,0:T(8,128)(2,1)} %bitcast.8), channel_id=1, source_target_pairs={{0,16},{1,17},{2,18},{3,19},{4,20},{5,21},{6,22},{7,23},{8,24},{9,... | collective-permute-start | bytes 1179656 | tf_op jit(solution)/shard_map/ppermute | solution.py:418
  5.2 7.9 %collective-permute-done.5.refs_1_ = bf16[192,1024]{1,0:T(8,128)(2,1)} collective-permute-done((bf16[192,1024]{1,0:T(8,128)(2,1)}, bf16[192,1024]{1,0:T(8,128)(2,1)}, u32[]{:S(2)}, u32[]{:S(2)}) %collective-permute-start.5) | collective-permute-done | bytes 393248 | tf_op jit(solution)/shard_map/ppermute | solution.py:418
  13.1 1.8 %collective-permute-start.7 = (bf16[192,1024]{1,0:T(8,128)(2,1)}, bf16[192,1024]{1,0:T(8,128)(2,1)}, u32[]{:S(2)}, u32[]{:S(2)}) collective-permute-start(bf16[192,1024]{1,0:T(8,128)(2,1)} %collective-permute-done.5.refs_1_), channel_id=1, source_target_pairs={{0,16},{1,17},{2,18},{3,19},{4,20},{5,21},{6,22},{7,23},{8,24},{9,... | collective-permute-start | bytes 1179656 | tf_op jit(solution)/shard_map/ppermute | solution.py:418
  14.9 3.3 %shard_map.119 = (f32[8,6,64,128]{3,2,1,0:T(8,128)S(1)}, f32[8,6,32,128]{3,2,1,0:T(8,128)S(1)}, f32[2,1152]{1,0:T(2,128)S(1)}, f32[6,32,128]{2,1,0:T(8,128)S(1)}, f32[6,32,32]{2,1,0:T(8,128)S(1)}) custom-call(s32[6]{0:T(128)} %len_hbm.1, s32[6]{0:T(128)} %off_hbm.1, bf16[6,32,2048]{2,1,0:T(8,128)(2,1)} %acts_hbm.1, f32[32,1024]{1,0:T(8,128)} %k_hbm.1), custom_call_target="tpu_custom_call" | custom-call | flops 25165824 | bytes 917552 | tf_op jit(solution)/shard_map/pallas_call | solution.py:389
  18.1 0.1 collective-permute-start
  18.2 3.1 %collective-permute-done = f32[2,1152]{1,0:T(2,128)S(1)} collective-permute-done((f32[2,1152]{1,0:T(2,128)S(1)}, f32[2,1152]{1,0:T(2,128)S(1)}, u32[]{:S(2)}, u32[]{:S(2)}) %collective-permute-start) | collective-permute-done | bytes 9248 | tf_op jit(solution)/shard_map/ppermute | solution.py:418
  21.3 2.5 %collective-permute-start.1 = (f32[2,1152]{1,0:T(2,128)S(1)}, f32[2,1152]{1,0:T(2,128)S(1)}, u32[]{:S(2)}, u32[]{:S(2)}) collective-permute-start(f32[2,1152]{1,0:T(2,128)S(1)} %add.19), channel_id=1, source_target_pairs={{0,6},{1,7},{2,4},{3,5},{4,2},{5,3},{6,0},{7,1},{8,14},{9,15},{10,... | collective-permute-start | bytes 27656 | tf_op jit(solution)/shard_map/ppermute | solution.py:418
  23.8 1.4 %collective-permute-done.1 = f32[2,1152]{1,0:T(2,128)S(1)} collective-permute-done((f32[2,1152]{1,0:T(2,128)S(1)}, f32[2,1152]{1,0:T(2,128)S(1)}, u32[]{:S(2)}, u32[]{:S(2)}) %collective-permute-start.1) | collective-permute-done | bytes 9248 | tf_op jit(solution)/shard_map/ppermute | solution.py:418
  25.3 1.4 %collective-permute-start.2 = (f32[2,1152]{1,0:T(2,128)S(1)}, f32[2,1152]{1,0:T(2,128)S(1)}, u32[]{:S(2)}, u32[]{:S(2)}) collective-permute-start(f32[2,1152]{1,0:T(2,128)S(1)} %add.20), channel_id=1, source_target_pairs={{0,12},{1,13},{2,14},{3,15},{4,8},{5,9},{6,10},{7,11},{8,4},{9,5},... | collective-permute-start | bytes 27656 | tf_op jit(solution)/shard_map/ppermute | solution.py:418
  26.7 1.6 %collective-permute-done.2 = f32[2,1152]{1,0:T(2,128)S(1)} collective-permute-done((f32[2,1152]{1,0:T(2,128)S(1)}, f32[2,1152]{1,0:T(2,128)S(1)}, u32[]{:S(2)}, u32[]{:S(2)}) %collective-permute-start.2) | collective-permute-done | bytes 9248 | tf_op jit(solution)/shard_map/ppermute | solution.py:418
  28.4 0.5 collective-permute-start.3
  28.8 2.6 %collective-permute-done.3 = f32[2,1152]{1,0:T(2,128)S(1)} collective-permute-done((f32[2,1152]{1,0:T(2,128)S(1)}, f32[2,1152]{1,0:T(2,128)S(1)}, u32[]{:S(2)}, u32[]{:S(2)}) %collective-permute-start.3) | collective-permute-done | bytes 9248 | tf_op jit(solution)/shard_map/ppermute | solution.py:418
  31.5 0.4 collective-permute-start.4
  31.8 0.8 %collective-permute-done.4 = f32[2,1152]{1,0:T(2,128)S(1)} collective-permute-done((f32[2,1152]{1,0:T(2,128)S(1)}, f32[2,1152]{1,0:T(2,128)S(1)}, u32[]{:S(2)}, u32[]{:S(2)}) %collective-permute-start.4) | collective-permute-done | bytes 9248 | tf_op jit(solution)/shard_map/ppermute | solution.py:418
  32.7 0.7 copy-done.4
  33.4 0.7 copy-done.6
  34.0 1.1 %shard_map.120.hid_ref = bf16[8,192,128]{2,1,0:T(8,128)(2,1)} custom-call(f32[2,1152]{1,0:T(2,128)S(1)} %add.23.st_ref, f32[8,128]{1,0:T(8,128)S(1)} %bitcast.13, f32[8,128]{1,0:T(8,128)S(1)} %bitcast.16, f32[6,32,128]{2,1,0:T(8,128)S(1)} %get-tuple-element.15.ok_ref, f32[8,6,32,128]{3,2,1,0:T(8,128)S(1)} %get-tuple-element.16.cv_ref), custom_call_target="tpu_custom_call" | custom-call | bytes 902144 | tf_op jit(solution)/shard_map/pallas_call | solution.py:389
  35.2 3.5 %all-to-all-start = ((bf16[8,192,128]{2,1,0:T(8,128)(2,1)}), bf16[8,192,128]{2,1,0:T(8,128)(2,1)S(1)}, u32[]{:S(2)}, u32[]{:S(2)}) async-start(bf16[8,192,128]{2,1,0:T(8,128)(2,1)} %shard_map.120.hid_ref), calls=%async_computation | async-start | bytes 786432 | tf_op jit(solution)/shard_map/all_to_all | solution.py:479
  38.7 0.4 collective-permute-start.8
  39.1 0.2 collective-permute-start.9
  39.2 0.3 collective-permute-start.10
  39.6 0.2 collective-permute-start.11
  39.8 0.7 shard_map.127.refs_3_
  40.4 0.7 shard_map.126.refs_2_
  41.1 0.0 copy-start
  41.1 0.0 copy-start.5
  41.1 0.7 shard_map.125.refs_1_
  41.8 0.7 shard_map.124.refs_0_
  42.5 0.2 copy-done
  42.7 4.3 %shard_map.128 = f32[8,112,128]{2,1,0:T(8,128)S(1)} custom-call(f32[2,1152]{1,0:T(2,128)S(1)} %add.23.st_ref, f32[8,128]{1,0:T(8,128)S(1)} %bitcast.14, f32[8,128]{1,0:T(8,128)S(1)} %bitcast.17, f32[6,32,128]{2,1,0:T(8,128)S(1)} %get-tuple-element.15.ok_ref, f32[8,6,64,128]{3,2,1,0:T(8,128)S(1)} %get-tuple-element.17.gp_ref, ...), custom_call_target="tpu_custom_call" | custom-call | flops 427819008 | bytes 5227520 | tf_op jit(solution)/shard_map/pallas_call | solution.py:389
  47.0 0.8 copy-done.3
  47.8 4.1 %all-to-all-start.1 = ((f32[8,112,128]{2,1,0:T(8,128)}), f32[8,112,128]{2,1,0:T(8,128)S(1)}, u32[]{:S(2)}, u32[]{:S(2)}) async-start(f32[8,112,128]{2,1,0:T(8,128)} %copy-done.3), calls=%async_computation.1 | async-start | bytes 917504 | tf_op jit(solution)/shard_map/all_to_all | solution.py:488
  51.8 0.1 pad_add_fusion.at_ref
  51.9 3.1 %shard_map.123 = bf16[4,128,128]{2,1,0:T(8,128)(2,1)} custom-call(s32[2]{0:T(128)S(1)} %pad_add_fusion.at_ref, bf16[8,192,128]{2,1,0:T(8,128)(2,1)S(1)} %all-to-all-done.recv_ref, bf16[192,1024]{1,0:T(8,128)(2,1)S(1)} %bitcast.11, bf16[192,1024]{1,0:T(8,128)(2,1)} %collective-permute-done.5.refs_1_, bf16[192,1024]{1,0:T(8,128)(2,1)} %collective-permute-done.6.refs_2_, ...), custom_call_target="tpu_custom_call" | custom-call | flops 201326592 | bytes 3538944 | tf_op jit(solution)/shard_map/pallas_call | solution.py:389
  55.0 0.0 copy-start.1
  55.0 1.6 %collective-permute-start.12 = (bf16[4,128,128]{2,1,0:T(8,128)(2,1)}, bf16[4,128,128]{2,1,0:T(8,128)(2,1)}, u32[]{:S(2)}, u32[]{:S(2)}) collective-permute-start(bf16[4,128,128]{2,1,0:T(8,128)(2,1)} %shard_map.123), channel_id=1, source_target_pairs={{0,1},{1,0},{2,3},{3,2},{4,5},{5,4},{6,7},{7,6},{8,9},{9,8},{10,11... | collective-permute-start | bytes 393224 | tf_op jit(solution)/shard_map/ppermute | solution.py:418
  56.7 2.4 %shard_map.122.own_ref = bf16[4,128,128]{2,1,0:T(8,128)(2,1)S(1)} custom-call(s32[2]{0:T(128)S(1)} %pad_add_fusion.at_ref, bf16[8,192,128]{2,1,0:T(8,128)(2,1)S(1)} %all-to-all-done.recv_ref, bf16[192,1024]{1,0:T(8,128)(2,1)S(1)} %bitcast.12, bf16[192,1024]{1,0:T(8,128)(2,1)} %collective-permute-done.5.refs_1_, ...), custom_call_target="tpu_custom_call" | custom-call | flops 201326592 | bytes 3538944 | tf_op jit(solution)/shard_map/pallas_call | solution.py:389
  59.1 1.8 %all-to-all-done.1.lags_ref = f32[8,112,128]{2,1,0:T(8,128)S(1)} async-done(((f32[8,112,128]{2,1,0:T(8,128)}), f32[8,112,128]{2,1,0:T(8,128)S(1)}, u32[]{:S(2)}, u32[]{:S(2)}) %all-to-all-start.1) | async-done | bytes 458784 | tf_op jit(solution)/shard_map/all_to_all | solution.py:488
  60.8 0.5 collective-permute-done.12.recv_ref
  61.3 1.0 %shard_map.129.own_ref = bf16[736,128]{1,0:T(8,128)(2,1)S(1)} custom-call(bf16[4,128,128]{2,1,0:T(8,128)(2,1)S(1)} %shard_map.122.own_ref, bf16[4,128,128]{2,1,0:T(8,128)(2,1)} %collective-permute-done.12.recv_ref, f32[8,112,128]{2,1,0:T(8,128)S(1)} %all-to-all-done.1.lags_ref), custom_call_target="tpu_custom_call" | custom-call | bytes 720896 | tf_op jit(solution)/shard_map/pallas_call | solution.py:389
  62.3 2.7 %collective-permute-start.13 = (bf16[736,128]{1,0:T(8,128)(2,1)S(1)}, bf16[736,128]{1,0:T(8,128)(2,1)S(1)}, u32[]{:S(2)}, u32[]{:S(2)}) collective-permute-start(bf16[736,128]{1,0:T(8,128)(2,1)S(1)} %shard_map.129.own_ref), channel_id=1, source_target_pairs={{0,2},{1,3},{2,0},{3,1},{4,6},{5,7},{6,4},{7,5},{8,10},{9,11},{10,... | collective-permute-start | bytes 565256 | tf_op jit(solution)/shard_map/ppermute | solution.py:418
  65.0 8.6 %collective-permute-done.13.recv_ref = bf16[736,128]{1,0:T(8,128)(2,1)S(1)} collective-permute-done((bf16[736,128]{1,0:T(8,128)(2,1)S(1)}, bf16[736,128]{1,0:T(8,128)(2,1)S(1)}, u32[]{:S(2)}, u32[]{:S(2)}) %collective-permute-start.13) | collective-permute-done | bytes 188448 | tf_op jit(solution)/shard_map/ppermute | solution.py:418
  73.6 0.1 shard_map.130.own_ref
  73.6 0.7 collective-permute-start.14
  74.4 2.7 %shard_map.121 = bf16[6,32,1024]{2,1,0:T(8,128)(2,1)} custom-call(bf16[8,192,128]{2,1,0:T(8,128)(2,1)} %shard_map.120.hid_ref, bf16[1024,1024]{1,0:T(8,128)(2,1)S(1)} %copy-done.1), custom_call_target="tpu_custom_call" | custom-call | bytes 2490368 | tf_op jit(solution)/shard_map/pallas_call | solution.py:389
  77.1 2.2 %collective-permute-done.14.recv_ref = bf16[736,128]{1,0:T(8,128)(2,1)S(1)} collective-permute-done((bf16[736,128]{1,0:T(8,128)(2,1)S(1)}, bf16[736,128]{1,0:T(8,128)(2,1)S(1)}, u32[]{:S(2)}, u32[]{:S(2)}) %collective-permute-start.14) | collective-permute-done | bytes 188448 | tf_op jit(solution)/shard_map/ppermute | solution.py:418
  79.3 1.4 %shard_map.131 = (f32[128,1024]{1,0:T(8,128)}, f32[32,128]{1,0:T(8,128)}, f32[8,128]{1,0:T(8,128)}, f32[8,128]{1,0:T(8,128)}) custom-call(s32[2]{0:T(128)S(1)} %pad_add_fusion.at_ref, bf16[736,128]{1,0:T(8,128)(2,1)S(1)} %shard_map.130.own_ref, bf16[736,128]{1,0:T(8,128)(2,1)S(1)} %collective-permute-done.14.recv_ref, f32[2,1152]{1,0:T(2,128)S(1)} %add.23.st_ref, ...), custom_call_target="tpu_custom_call" | custom-call | bytes 390144 | tf_op jit(solution)/shard_map/pallas_call | solution.py:389
  (19 shorter events, 0.1 us)
Async XLA Ops:
  0.6 38.0 %copy-start.2 = (bf16[6,32,1024]{2,1,0:T(8,128)(2,1)S(1)}, bf16[6,32,1024]{2,1,0:T(8,128)(2,1)}, u32[]{:S(2)}) copy-start(bf16[6,32,1024]{2,1,0:T(8,128)(2,1)} %param.9) | copy-start | bytes 1179652
  0.6 12.5 %collective-permute-start.5 = (bf16[192,1024]{1,0:T(8,128)(2,1)}, bf16[192,1024]{1,0:T(8,128)(2,1)}, u32[]{:S(2)}, u32[]{:S(2)}) collective-permute-start(bf16[192,1024]{1,0:T(8,128)(2,1)} %bitcast.7), channel_id=1, source_target_pairs={{0,8},{1,9},{2,10},{3,11},{4,12},{5,13},{6,14},{7,15},{8,0},{9,1},... | collective-permute-start | bytes 1179656 | tf_op jit(solution)/shard_map/ppermute | solution.py:418
  3.7 35.6 %collective-permute-start.6 = (bf16[192,1024]{1,0:T(8,128)(2,1)}, bf16[192,1024]{1,0:T(8,128)(2,1)}, u32[]{:S(2)}, u32[]{:S(2)}) collective-permute-start(bf16[192,1024]{1,0:T(8,128)(2,1)} %bitcast.8), channel_id=1, source_target_pairs={{0,16},{1,17},{2,18},{3,19},{4,20},{5,21},{6,22},{7,23},{8,24},{9,... | collective-permute-start | bytes 1179656 | tf_op jit(solution)/shard_map/ppermute | solution.py:418
  13.1 26.5 %collective-permute-start.7 = (bf16[192,1024]{1,0:T(8,128)(2,1)}, bf16[192,1024]{1,0:T(8,128)(2,1)}, u32[]{:S(2)}, u32[]{:S(2)}) collective-permute-start(bf16[192,1024]{1,0:T(8,128)(2,1)} %collective-permute-done.5.refs_1_), channel_id=1, source_target_pairs={{0,16},{1,17},{2,18},{3,19},{4,20},{5,21},{6,22},{7,23},{8,24},{9,... | collective-permute-start | bytes 1179656 | tf_op jit(solution)/shard_map/ppermute | solution.py:418
  18.1 3.2 %collective-permute-start = (f32[2,1152]{1,0:T(2,128)S(1)}, f32[2,1152]{1,0:T(2,128)S(1)}, u32[]{:S(2)}, u32[]{:S(2)}) collective-permute-start(f32[2,1152]{1,0:T(2,128)S(1)} %get-tuple-element.14), channel_id=1, source_target_pairs={{0,5},{1,4},{2,7},{3,6},{4,1},{5,0},{6,3},{7,2},{8,13},{9,12},{10,... | collective-permute-start | bytes 27656 | tf_op jit(solution)/shard_map/ppermute | solution.py:418
  21.3 4.0 %collective-permute-start.1 = (f32[2,1152]{1,0:T(2,128)S(1)}, f32[2,1152]{1,0:T(2,128)S(1)}, u32[]{:S(2)}, u32[]{:S(2)}) collective-permute-start(f32[2,1152]{1,0:T(2,128)S(1)} %add.19), channel_id=1, source_target_pairs={{0,6},{1,7},{2,4},{3,5},{4,2},{5,3},{6,0},{7,1},{8,14},{9,15},{10,... | collective-permute-start | bytes 27656 | tf_op jit(solution)/shard_map/ppermute | solution.py:418
  25.3 3.1 %collective-permute-start.2 = (f32[2,1152]{1,0:T(2,128)S(1)}, f32[2,1152]{1,0:T(2,128)S(1)}, u32[]{:S(2)}, u32[]{:S(2)}) collective-permute-start(f32[2,1152]{1,0:T(2,128)S(1)} %add.20), channel_id=1, source_target_pairs={{0,12},{1,13},{2,14},{3,15},{4,8},{5,9},{6,10},{7,11},{8,4},{9,5},... | collective-permute-start | bytes 27656 | tf_op jit(solution)/shard_map/ppermute | solution.py:418
  28.4 3.1 %collective-permute-start.3 = (f32[2,1152]{1,0:T(2,128)S(1)}, f32[2,1152]{1,0:T(2,128)S(1)}, u32[]{:S(2)}, u32[]{:S(2)}) collective-permute-start(f32[2,1152]{1,0:T(2,128)S(1)} %add.21), channel_id=1, source_target_pairs={{0,20},{1,21},{2,22},{3,23},{4,16},{5,17},{6,18},{7,19},{8,28},{9,... | collective-permute-start | bytes 27656 | tf_op jit(solution)/shard_map/ppermute | solution.py:418
  31.5 1.2 %collective-permute-start.4 = (f32[2,1152]{1,0:T(2,128)S(1)}, f32[2,1152]{1,0:T(2,128)S(1)}, u32[]{:S(2)}, u32[]{:S(2)}) collective-permute-start(f32[2,1152]{1,0:T(2,128)S(1)} %add.22), channel_id=1, source_target_pairs={{0,4},{1,5},{2,6},{3,7},{4,0},{5,1},{6,2},{7,3},{8,12},{9,13},{10,... | collective-permute-start | bytes 27656 | tf_op jit(solution)/shard_map/ppermute | solution.py:418
  32.7 0.7 copy-start.4
  33.4 0.7 copy-start.6
  35.2 12.6 %all-to-all-start = ((bf16[8,192,128]{2,1,0:T(8,128)(2,1)}), bf16[8,192,128]{2,1,0:T(8,128)(2,1)S(1)}, u32[]{:S(2)}, u32[]{:S(2)}) async-start(bf16[8,192,128]{2,1,0:T(8,128)(2,1)} %shard_map.120.hid_ref), calls=%async_computation | async-start | bytes 786432 | tf_op jit(solution)/shard_map/all_to_all | solution.py:479
  38.7 13.3 %collective-permute-start.8 = (bf16[192,1024]{1,0:T(8,128)(2,1)S(1)}, bf16[192,1024]{1,0:T(8,128)(2,1)}, u32[]{:S(2)}, u32[]{:S(2)}) collective-permute-start(bf16[192,1024]{1,0:T(8,128)(2,1)S(1)} %bitcast.9), channel_id=1, source_target_pairs={{0,4},{1,5},{2,6},{3,7},{4,0},{5,1},{6,2},{7,3},{8,12},{9,13},{10,... | collective-permute-start | bytes 1179656 | tf_op jit(solution)/shard_map/ppermute | solution.py:418
  39.1 12.9 %collective-permute-start.9 = (bf16[192,1024]{1,0:T(8,128)(2,1)}, bf16[192,1024]{1,0:T(8,128)(2,1)}, u32[]{:S(2)}, u32[]{:S(2)}) collective-permute-start(bf16[192,1024]{1,0:T(8,128)(2,1)} %collective-permute-done.5.refs_1_), channel_id=1, source_target_pairs={{0,4},{1,5},{2,6},{3,7},{4,0},{5,1},{6,2},{7,3},{8,12},{9,13},{10,... | collective-permute-start | bytes 1179656 | tf_op jit(solution)/shard_map/ppermute | solution.py:418
  39.2 12.7 %collective-permute-start.10 = (bf16[192,1024]{1,0:T(8,128)(2,1)}, bf16[192,1024]{1,0:T(8,128)(2,1)}, u32[]{:S(2)}, u32[]{:S(2)}) collective-permute-start(bf16[192,1024]{1,0:T(8,128)(2,1)} %collective-permute-done.6.refs_2_), channel_id=1, source_target_pairs={{0,4},{1,5},{2,6},{3,7},{4,0},{5,1},{6,2},{7,3},{8,12},{9,13},{10,... | collective-permute-start | bytes 1179656 | tf_op jit(solution)/shard_map/ppermute | solution.py:418
  39.6 12.3 %collective-permute-start.11 = (bf16[192,1024]{1,0:T(8,128)(2,1)}, bf16[192,1024]{1,0:T(8,128)(2,1)}, u32[]{:S(2)}, u32[]{:S(2)}) collective-permute-start(bf16[192,1024]{1,0:T(8,128)(2,1)} %collective-permute-done.7.refs_3_), channel_id=1, source_target_pairs={{0,4},{1,5},{2,6},{3,7},{4,0},{5,1},{6,2},{7,3},{8,12},{9,13},{10,... | collective-permute-start | bytes 1179656 | tf_op jit(solution)/shard_map/ppermute | solution.py:418
  41.1 1.6 %copy-start = (bf16[1024,1024]{1,0:T(8,128)(2,1)S(1)}, bf16[1024,1024]{1,0:T(8,128)(2,1)}, u32[]{:S(2)}) copy-start(bf16[1024,1024]{1,0:T(8,128)(2,1)} %w_ref.3) | copy-start | bytes 6291460
  41.1 1.6 %copy-start.5 = (f32[1024]{0:T(1024)S(1)}, f32[1024]{0:T(1024)}, u32[]{:S(2)}) copy-start(f32[1024]{0:T(1024)} %param.13) | copy-start | bytes 12292
  47.0 0.8 copy-start.3
  47.8 13.1 %all-to-all-start.1 = ((f32[8,112,128]{2,1,0:T(8,128)}), f32[8,112,128]{2,1,0:T(8,128)S(1)}, u32[]{:S(2)}, u32[]{:S(2)}) async-start(f32[8,112,128]{2,1,0:T(8,128)} %copy-done.3), calls=%async_computation.1 | async-start | bytes 917504 | tf_op jit(solution)/shard_map/all_to_all | solution.py:488
  55.0 19.4 %copy-start.1 = (bf16[1024,1024]{1,0:T(8,128)(2,1)S(1)}, bf16[1024,1024]{1,0:T(8,128)(2,1)}, u32[]{:S(2)}) copy-start(bf16[1024,1024]{1,0:T(8,128)(2,1)} %w_ref.3) | copy-start | bytes 6291460
  55.0 6.3 %collective-permute-start.12 = (bf16[4,128,128]{2,1,0:T(8,128)(2,1)}, bf16[4,128,128]{2,1,0:T(8,128)(2,1)}, u32[]{:S(2)}, u32[]{:S(2)}) collective-permute-start(bf16[4,128,128]{2,1,0:T(8,128)(2,1)} %shard_map.123), channel_id=1, source_target_pairs={{0,1},{1,0},{2,3},{3,2},{4,5},{5,4},{6,7},{7,6},{8,9},{9,8},{10,11... | collective-permute-start | bytes 393224 | tf_op jit(solution)/shard_map/ppermute | solution.py:418
  62.3 11.3 %collective-permute-start.13 = (bf16[736,128]{1,0:T(8,128)(2,1)S(1)}, bf16[736,128]{1,0:T(8,128)(2,1)S(1)}, u32[]{:S(2)}, u32[]{:S(2)}) collective-permute-start(bf16[736,128]{1,0:T(8,128)(2,1)S(1)} %shard_map.129.own_ref), channel_id=1, source_target_pairs={{0,2},{1,3},{2,0},{3,1},{4,6},{5,7},{6,4},{7,5},{8,10},{9,11},{10,... | collective-permute-start | bytes 565256 | tf_op jit(solution)/shard_map/ppermute | solution.py:418
  73.6 5.7 %collective-permute-start.14 = (bf16[736,128]{1,0:T(8,128)(2,1)S(1)}, bf16[736,128]{1,0:T(8,128)(2,1)S(1)}, u32[]{:S(2)}, u32[]{:S(2)}) collective-permute-start(bf16[736,128]{1,0:T(8,128)(2,1)S(1)} %shard_map.130.own_ref), channel_id=1, source_target_pairs={{0,1},{1,0},{2,3},{3,2},{4,5},{5,4},{6,7},{7,6},{8,9},{9,8},{10,11... | collective-permute-start | bytes 565256 | tf_op jit(solution)/shard_map/ppermute | solution.py:418
